TPU v7x, 512 devices: a whole 4x8x8 slice. The times are simulated.
512 devices in a mesh: tm: 8 (over x, core), azim: 64 (over z, y).
Axes of the slice: x: 4, y: 8, z: 8, core: 2. Of those that a mesh axis runs over, the one named last changes fastest.
Arguments:
- pressure: bfloat16 [256, 160, 1024], P('azim', None, 'tm'), may hold values from -6 to 6
Outputs:
- gram_xx: float32 [128, 2, 1024, 1024], P('azim', None, 'tm')
- gram_xy: float32 [128, 2, 1024, 1024], P('azim', None, 'tm')
All inputs are finite; a program needn't handle non-finite values.
Results may differ from a plain program's by a relative error of at most 0.0046.
Values may be sent and summed in bfloat16 or wider, within the bound.
No kernel may reach another device: no remote copies, remote signals or barrier semaphores. Data moves between devices by JAX's collectives and lax.ppermute only.
A program may use at most 64 MiB of HBM per device.

v0:
```python
import jax
import jax.numpy as jnp
from jax import lax
from jax.sharding import PartitionSpec as P

THETA = 256
MODES = 128
ROWS = 160


def from_behind(array, axis, by):
    peers = lax.axis_size(axis)
    pairs = [(i, i + by) for i in range(peers) if 0 <= i + by < peers]
    return lax.ppermute(array, axis, pairs)


def make_table(parts):
    per_set = MODES // parts
    column = jnp.arange(2 * MODES, dtype=jnp.int32)
    owner = column // (2 * per_set)
    within = column % (2 * per_set)
    imag_flag = within // per_set
    wave = owner * per_set + within % per_set
    angle_idx = jnp.arange(THETA, dtype=jnp.int32)[:, None]
    phase = (angle_idx * wave[None, :] % THETA).astype(jnp.float32) * (2.0 * jnp.pi / THETA)
    scale = THETA ** (-0.5)
    values = jnp.where(imag_flag[None, :] == 1, -jnp.sin(phase), jnp.cos(phase)) * scale
    return values.astype(jnp.bfloat16)


def complex_tiles(left_cat, right, gain):
    width = right.shape[3]
    half = left_cat.shape[2] // 2
    right_cat = jnp.transpose(right, (1, 2, 0, 3)).reshape(
        right.shape[1], right.shape[2], 2 * width
    )
    product = jnp.einsum("jrs,jru->jsu", left_cat, right_cat, preferred_element_type=jnp.float32)
    real = product[:, :half, :width] + product[:, half:, width:]
    imag = product[:, :half, width:] - product[:, half:, :width]
    return jnp.stack([real, imag], axis=1) * gain


def body(pressure):
    parts = lax.axis_size("azim")
    snap_dev = pressure.shape[2]
    table = make_table(parts)
    spectrum = jnp.einsum(
        "art,ac->crt",
        lax.all_to_all(pressure, "azim", split_axis=2, concat_axis=0, tiled=True),
        table,
        preferred_element_type=jnp.float32,
    ).astype(jnp.bfloat16)
    owned = lax.all_to_all(spectrum, "azim", split_axis=0, concat_axis=2, tiled=True)
    modes = owned.reshape(2, owned.shape[0] // 2, owned.shape[1], owned.shape[2])
    per_set = modes.shape[1]
    depth = modes.shape[2]
    gain = ROWS ** (-0.5)
    left_cat = jnp.transpose(modes, (1, 2, 0, 3)).reshape(per_set, depth, 2 * snap_dev)
    limit = (lax.axis_index("tm") + 1) * snap_dev

    def place(tile):
        columns = jnp.arange(tile.shape[3], dtype=jnp.int32)
        tile = jnp.where((columns < limit)[None, None, None, :], tile, jnp.float32(0.0))
        return tile

    following = from_behind(modes[..., :1], "tm", -1)
    successor = jnp.concatenate([modes[..., 1:], following], axis=3)
    block_x = lax.all_gather(modes, "tm", axis=3, tiled=True)
    block_y = lax.all_gather(successor, "tm", axis=3, tiled=True)
    gram_xx = place(complex_tiles(left_cat, block_x, gain))
    gram_xy = place(complex_tiles(left_cat, block_y, gain))
    return (gram_xx, gram_xy)


def solution(mesh):
    in_specs = (P("azim", None, "tm"),)
    out_specs = (P("azim", None, "tm", None), P("azim", None, "tm", None))
    return jax.shard_map(body, mesh=mesh, in_specs=in_specs, out_specs=out_specs, check_vma=False)
```

profile of v0, /device:TPU:1, one launch (start us, length us, event | category | flops | bytes accessed | tf_op | source)
XLA Modules:
  0.0 138.6 jit_solution(5540411087914678155)
XLA Ops:
  7.2 1.8 %copy.16 = bf16[4,160,128]{1,0,2:T(4,128)(2,1)} copy(bf16[4,160,128]{2,1,0:T(8,128)(2,1)} %param.1) | data formatting | bytes 327680 | tf_op args[0]
  8.9 17.1 %all-to-all-start = ((bf16[4,160,128]{1,0,2:T(4,128)(2,1)}), bf16[4,160,128]{1,0,2:T(4,128)(2,1)S(1)}, u32[]{:S(2)}, u32[]{:S(2)}) async-start(bf16[4,160,128]{1,0,2:T(4,128)(2,1)} %copy.16), calls=%async_computation | async-start | bytes 524288 | tf_op jit(solution)/shard_map/all_to_all | solution.py:49
  26.1 0.0 all-gather.3.cloned.1.call-start
  26.2 12.8 %all-to-all-done = bf16[4,160,128]{1,0,2:T(4,128)(2,1)S(1)} async-done(((bf16[4,160,128]{1,0,2:T(4,128)(2,1)}), bf16[4,160,128]{1,0,2:T(4,128)(2,1)S(1)}, u32[]{:S(2)}, u32[]{:S(2)}) %all-to-all-start) | async-done | bytes 163872 | tf_op jit(solution)/shard_map/all_to_all | solution.py:49
  38.9 0.2 copy.17
  39.1 1.3 convolution_convert_fusion
  40.4 0.2 copy.19
  40.6 17.9 %all_to_all.33 = bf16[256,160,2]{1,2,0:T(2,128)(2,1)S(1)} all-to-all(bf16[256,160,2]{1,2,0:T(2,128)(2,1)S(1)} %copy.19), channel_id=1, replica_groups=mesh['tm'=8,'azim'=64] {'azim'}, dimensions={0} | all-to-all | bytes 327680 | tf_op jit(solution)/shard_map/all_to_all | solution.py:53
  58.5 0.2 copy.20
  58.7 0.9 reshape.74
  59.7 0.0 all-gather.3.cloned.1.call-update
  59.7 0.0 all-gather.5.cloned.1.call-start
  59.7 0.7 slice.45
  60.5 5.4 %collective-permute-start = (bf16[2,2,160,1]{2,3,1,0:T(2,128)(2,1)S(1)}, bf16[2,2,160,1]{2,3,1,0:T(2,128)(2,1)S(1)}, u32[]{:S(2)}, u32[]{:S(2)}) collective-permute-start(bf16[2,2,160,1]{2,3,1,0:T(2,128)(2,1)S(1)} %slice.45), channel_id=1, source_target_pairs={{64,0},{128,64},{192,128},{256,192},{320,256},{384,320},{448,384},... | collective-permute-start | bytes 3848 | tf_op jit(solution)/shard_map/ppermute | solution.py:14
  65.9 1.0 slice.44
  66.9 1.4 collective-permute-done
  68.3 0.8 pad_maximum_fusion
  69.0 0.0 all-gather.5.cloned.1.call-update
  69.0 1.1 copy.21
  70.2 0.1 reshape.75
  70.3 15.5 %all-gather.3.cloned.1.call-done = bf16[2,2,160,1024]{2,3,1,0:T(8,128)(2,1)} async-done(((bf16[2,2,160,128]{2,3,1,0:T(8,128)(2,1)}), bf16[2,2,160,1024]{2,3,1,0:T(8,128)(2,1)}) %all-gather.3.cloned.1.call-update) | async-done | bytes 1310736 | tf_op jit(solution)/shard_map/all_gather | solution.py:68
  85.8 4.2 %copy.22 = bf16[2,160,2,1024]{3,2,1,0:T(2,128)(2,1)S(1)} copy(bf16[2,160,2,1024]{1,3,0,2:T(8,128)(2,1)} %bitcast.28) | data formatting | bytes 2621440 | tf_op jit(solution)/shard_map/transpose | solution.py:34
  90.0 1.0 reshape.76
  91.0 2.7 %fusion.31 = f32[2,256,2048]{2,1,0:T(8,128)} fusion(bf16[2,160,256]{2,1,0:T(8,128)(2,1)S(1)} %reshape.75, bf16[2,160,2048]{2,1,0:T(8,128)(2,1)S(1)} %reshape.76), kind=kOutput, calls=%fused_computation.55 | convolution fusion | flops 335544320 | bytes 5668864 | tf_op jit(solution)/shard_map/jrs,jru->jsu/dot_general | solution.py:37
  93.7 25.8 %all-gather.5.cloned.1.call-done = bf16[2,2,160,1024]{2,3,1,0:T(8,128)(2,1)} async-done(((bf16[2,2,160,128]{2,3,1,0:T(8,128)(2,1)}), bf16[2,2,160,1024]{2,3,1,0:T(8,128)(2,1)}) %all-gather.5.cloned.1.call-update) | async-done | bytes 1310736 | tf_op jit(solution)/shard_map/all_gather | solution.py:69
  119.5 4.2 %copy.23 = bf16[2,160,2,1024]{3,2,1,0:T(2,128)(2,1)S(1)} copy(bf16[2,160,2,1024]{1,3,0,2:T(8,128)(2,1)} %bitcast.29) | data formatting | bytes 2621440 | tf_op jit(solution)/shard_map/transpose | solution.py:34
  123.7 1.0 reshape.77
  124.7 0.0 copy-start
  124.7 0.8 fusion.32
  125.5 1.4 %copy-done = f32[2,256,2048]{2,1,0:T(8,128)S(1)} copy-done((f32[2,256,2048]{2,1,0:T(8,128)S(1)}, f32[2,256,2048]{2,1,0:T(8,128)}, u32[]{:S(2)}) %copy-start) | copy-done | bytes 4194328
  126.9 1.4 fusion.3
  128.3 0.6 fusion.1
  128.9 1.5 %copy.24 = f32[2,2,128,1024]{3,2,1,0:T(8,128)} copy(f32[2,2,128,1024]{3,2,0,1:T(8,128)S(1)} %get-tuple-element.13) | data formatting | bytes 4194304
  130.3 1.5 %copy.25 = f32[2,2,128,1024]{3,2,1,0:T(8,128)} copy(f32[2,2,128,1024]{3,2,0,1:T(8,128)S(1)} %get-tuple-element.12) | data formatting | bytes 4194304
  (3 shorter events, 0.0 us)
Async XLA Ops:
  8.9 30.0 %all-to-all-start = ((bf16[4,160,128]{1,0,2:T(4,128)(2,1)}), bf16[4,160,128]{1,0,2:T(4,128)(2,1)S(1)}, u32[]{:S(2)}, u32[]{:S(2)}) async-start(bf16[4,160,128]{1,0,2:T(4,128)(2,1)} %copy.16), calls=%async_computation | async-start | bytes 524288 | tf_op jit(solution)/shard_map/all_to_all | solution.py:49
  26.1 59.7 %all-gather.3.cloned.1.call-start = ((), (), s32[]{:S(2)}) async-start(), calls=%async_computation.2 | async-start | bytes 2359296 | tf_op jit(solution)/shard_map/all_gather | solution.py:68
  59.7 59.8 %all-gather.5.cloned.1.call-start = ((), (), s32[]{:S(2)}) async-start(), calls=%async_computation.3 | async-start | bytes 2359296 | tf_op jit(solution)/shard_map/all_gather | solution.py:69
  60.5 7.8 %collective-permute-start = (bf16[2,2,160,1]{2,3,1,0:T(2,128)(2,1)S(1)}, bf16[2,2,160,1]{2,3,1,0:T(2,128)(2,1)S(1)}, u32[]{:S(2)}, u32[]{:S(2)}) collective-permute-start(bf16[2,2,160,1]{2,3,1,0:T(2,128)(2,1)S(1)} %slice.45), channel_id=1, source_target_pairs={{64,0},{128,64},{192,128},{256,192},{320,256},{384,320},{448,384},... | collective-permute-start | bytes 3848 | tf_op jit(solution)/shard_map/ppermute | solution.py:14
  124.7 2.2 %copy-start = (f32[2,256,2048]{2,1,0:T(8,128)S(1)}, f32[2,256,2048]{2,1,0:T(8,128)}, u32[]{:S(2)}) copy-start(f32[2,256,2048]{2,1,0:T(8,128)} %fusion.31) | copy-start | bytes 12582916
Sparse Core Ops, SparseCore 0:
  59.8 25.9 all-gather.2
  88.5 30.9 all-gather.4
where the time goes:
time: 139 us
  waiting for transfers between devices  55.4 us (40%)
  starting transfers between devices  22.6 us (16%)
  local copies, waits for them, and re-layouts  21 us (15%)
  blocking collectives  17.9 us (13%)
  between operations  14.2 us (10%)
  matrix products  4.74 us (3%)
  other arithmetic  2.69 us (2%)
    all_gather x1, waiting for transfers between devices, body(): block_y = lax.all_gather(successor, 'tm', axis=3, tiled=True)  25.8 us
    all_to_all x1, blocking collectives, body(): lax.all_to_all(spectrum, 'azim', split_axis=0, concat_axis=2, tiled=True)  17.9 us
    all_to_all x1, starting transfers between devices, body(): lax.all_to_all(pressure, 'azim', split_axis=2, concat_axis=0, tiled=True)  17.1 us
    all_gather x1, waiting for transfers between devices, body(): block_x = lax.all_gather(modes, 'tm', axis=3, tiled=True)  15.5 us
    all_to_all x1, waiting for transfers between devices, body(): lax.all_to_all(pressure, 'azim', split_axis=2, concat_axis=0, tiled=True)  12.8 us
    transpose x2, local copies, waits for them, and re-layouts, complex_tiles(): jnp.transpose(right, (1, 2, 0, 3))  8.39 us
    unnamed x5, local copies, waits for them, and re-layouts  6.12 us
    ppermute x1, starting transfers between devices, from_behind(): return lax.ppermute(array, axis, pairs)  5.41 us
  transfers between devices with their start and end apart: 4, of which 4 were waited for; matrix products, arithmetic and copies ran while one was open for 8% of the time, Pallas kernels for 0%

commit v1 on v0

v1 whole, which is shorter than its diff:
```python
import jax
import jax.numpy as jnp
import numpy as np
from jax import lax
from jax.experimental import pallas as pl
from jax.experimental.pallas import tpu as pltpu
from jax.sharding import PartitionSpec as P

THETA = 256
MODES = 128
ROWS = 160
LANES = 128
HALF = 64
PARTS = 64
FIVE = 5
CELL = 2 * FIVE


def make_table():
    b, alo, p, k, ahi, s = np.meshgrid(
        np.arange(2), np.arange(2), np.arange(2), np.arange(64), np.arange(2), np.arange(64), indexing="ij"
    )
    angle = 4 * s + 2 * ahi + alo
    wave = 2 * k + b
    phase = ((angle * wave) % THETA).astype(np.float32) * np.float32(2.0 * np.pi / THETA)
    values = np.where(p == 1, -np.sin(phase), np.cos(phase)) * np.float32(THETA ** (-0.5))
    return values.astype(np.float32).reshape(512, 128).astype(jnp.bfloat16)


def low_lanes(shape):
    return lax.broadcasted_iota(jnp.int32, shape, 1) < HALF


def spread_kernel(x_ref, o_ref, scr):
    low = low_lanes((ROWS, LANES))
    for ahi in range(2):
        even = x_ref[2 * ahi].astype(jnp.float32)
        odd = x_ref[2 * ahi + 1].astype(jnp.float32)
        scr[pl.ds(ahi, ROWS, stride=2), :] = jnp.where(low, even, pltpu.roll(odd, HALF, 1))
        scr[pl.ds(2 * ROWS + ahi, ROWS, stride=2), :] = jnp.where(low, pltpu.roll(even, HALF, 1), odd)
    o_ref[...] = scr[...].astype(jnp.bfloat16)


def transform_kernel(x_ref, t_ref, o_ref, scr_in, scr_out):
    scr_in[...] = x_ref[...].astype(jnp.float32)
    low = low_lanes((LANES, LANES))
    for r5 in range(FIVE):
        field = jnp.concatenate(
            [scr_in[pl.ds(2 * r5 + ahi, PARTS, stride=CELL), :] for ahi in range(2)], axis=0
        ).astype(jnp.bfloat16)
        y = jnp.dot(t_ref[...], field, preferred_element_type=jnp.float32)
        straight = jnp.where(low, y[0:128], y[384:512])
        crossed = jnp.where(low, y[256:384], y[128:256])
        both = straight + pltpu.roll(crossed, HALF, 1)
        for p in range(2):
            scr_out[pl.ds(2 * r5 + p, PARTS, stride=CELL), :] = both[64 * p : 64 * p + 64]
    o_ref[...] = scr_out[...].astype(jnp.bfloat16)


def gram_kernel(idx_ref, a_ref, b_ref, xx_ref, xy_ref, right, left):
    step = pl.program_id(0)
    tm = idx_ref[0]
    core = lax.rem(tm, 2)

    @pl.when(step == 0)
    def _():
        low = low_lanes((2 * ROWS, LANES))
        for own, ref in ((True, a_ref), (False, b_ref)):
            par = core if own else 1 - core
            for x in range(4):
                first = ref[x, 0 : 2 * ROWS].astype(jnp.float32)
                second = ref[x, 2 * ROWS : 4 * ROWS].astype(jnp.float32)
                at = pl.multiple_of((2 * x + par) * LANES, LANES)
                right[0, :, pl.ds(at, LANES)] = jnp.where(low, first, pltpu.roll(second, HALF, 1)).astype(jnp.bfloat16)
                right[1, :, pl.ds(at, LANES)] = jnp.where(low, pltpu.roll(first, HALF, 1), second).astype(jnp.bfloat16)
        even = lax.rem(lax.broadcasted_iota(jnp.int32, (2 * ROWS, LANES), 0), 2) == 0
        here = pl.multiple_of(tm * LANES, LANES)
        for m in range(2):
            f = right[m, :, pl.ds(here, LANES)].astype(jnp.float32)
            turned = jnp.where(even, -pltpu.roll(f, 2 * ROWS - 1, 0), pltpu.roll(f, 1, 0))
            left[2 * m] = f.T.astype(jnp.bfloat16)
            left[2 * m + 1] = turned.T.astype(jnp.bfloat16)

    g = jnp.dot(left[step], right[step // 2], preferred_element_type=jnp.float32) * jnp.float32(ROWS ** (-0.5))
    col = lax.broadcasted_iota(jnp.int32, g.shape, 1)
    keep = col < (tm + 1) * LANES
    xx_ref[0, 0] = jnp.where(keep, g, 0.0)
    xy_ref[0, 0] = jnp.where(keep & (col < g.shape[1] - 1), pltpu.roll(g, g.shape[1] - 1, 1), 0.0)


def body(pressure):
    f32 = jnp.float32
    bf16 = jnp.bfloat16
    tm = lax.axis_index("tm")
    send = pl.pallas_call(
        spread_kernel,
        out_shape=jax.ShapeDtypeStruct((640, LANES), bf16),
        scratch_shapes=[pltpu.VMEM((640, LANES), f32)],
        name="spread",
    )(pressure)
    got = lax.all_to_all(send.reshape(PARTS, FIVE, 2, LANES), "azim", 0, 0, tiled=True)
    spectrum = pl.pallas_call(
        transform_kernel,
        out_shape=jax.ShapeDtypeStruct((640, LANES), bf16),
        scratch_shapes=[pltpu.VMEM((640, LANES), f32), pltpu.VMEM((640, LANES), f32)],
        name="transform",
    )(got.reshape(640, LANES), jnp.asarray(make_table()))
    owned = lax.all_to_all(spectrum.reshape(PARTS, FIVE, 2, LANES), "azim", 0, 0, tiled=True)
    owned = owned.reshape(640, LANES)
    chips = [[2 * x + c for x in range(4)] for c in range(2)]
    mine = lax.all_to_all(
        jnp.broadcast_to(owned[None], (4, 640, LANES)), "tm", 0, 0, tiled=True, axis_index_groups=chips
    )
    theirs = lax.ppermute(mine, "tm", [(i, i ^ 1) for i in range(8)])
    out = jax.ShapeDtypeStruct((2, 2, LANES, 1024), f32)
    block = pl.BlockSpec((1, 1, LANES, 1024), lambda i, idx: (i // 2, i % 2, 0, 0))
    whole = pl.BlockSpec((4, 640, LANES), lambda i, idx: (0, 0, 0))
    return pl.pallas_call(
        gram_kernel,
        grid_spec=pltpu.PrefetchScalarGridSpec(
            num_scalar_prefetch=1,
            grid=(4,),
            in_specs=[whole, whole],
            out_specs=[block, block],
            scratch_shapes=[pltpu.VMEM((2, 2 * ROWS, 1024), bf16), pltpu.VMEM((4, LANES, 2 * ROWS), bf16)],
        ),
        out_shape=(out, out),
        name="gram",
    )(tm.astype(jnp.int32).reshape(1), mine, theirs)


def solution(mesh):
    in_specs = (P("azim", None, "tm"),)
    out_specs = (P("azim", None, "tm", None), P("azim", None, "tm", None))
    return jax.shard_map(body, mesh=mesh, in_specs=in_specs, out_specs=out_specs, check_vma=False)
```

time: 139 us -> 76.3 us (0.55)
  waiting for transfers between devices: 55.4 us -> 1.7 us
  blocking collectives: 17.9 us -> 57 us
  local copies, waits for them, and re-layouts: 21 us -> 0.93 us
  starting transfers between devices: 22.6 us -> 6.86 us
  between operations: 14.2 us -> 0.65 us
  Pallas kernels: 0 us -> 8.85 us
  matrix products: 4.74 us -> 0 us
  other arithmetic: 2.69 us -> 0 us
    all_gather x2 -> x0, waiting for transfers between devices: 41.3 us -> none  [the longest x1 25.8 us: body(): block_y = lax.all_gather(successor, 'tm', axis=3, tiled=True)]
    all_to_all x1 -> x3, blocking collectives: 17.9 us -> 57 us  [the longest x1 29 us: body(): lax.all_to_all(send.reshape(PARTS, FIVE, 2, LANES), 'azim', 0, 0, tiled=T...]
    all_to_all x1 -> x0, starting transfers between devices: 17.1 us -> none  [body(): lax.all_to_all(pressure, 'azim', split_axis=2, concat_axis=0, tiled=True)]
    all_to_all x1 -> x0, waiting for transfers between devices: 12.8 us -> none  [body(): lax.all_to_all(pressure, 'azim', split_axis=2, concat_axis=0, tiled=True)]
    transpose x3 -> x0, local copies, waits for them, and re-layouts: 9.51 us -> none  [the longest x2 8.39 us: complex_tiles(): jnp.transpose(right, (1, 2, 0, 3))]
    pallas_call x0 -> x3, Pallas kernels: none -> 8.85 us  [the longest x1 5.06 us: body(): pl.pallas_call(gram_kernel, grid_spec=pltpu.PrefetchScalarGridSpec(num_sc...]
    unnamed x5 -> x4, local copies, waits for them, and re-layouts: 6.12 us -> 0.85 us
    dot_general x3 -> x0, matrix products: 4.74 us -> none  [the longest x2 3.47 us: complex_tiles(): jnp.einsum('jrs,jru->jsu', left_cat, right_cat, preferred_element_type=jn...]
  transfers between devices with their start and end apart: 4 -> 1, of which waited for: 4 -> 1; matrix products, arithmetic and copies ran while one was open for 8% -> 0% of each run, Pallas kernels for 0% -> 0%
where the time goes in v1:
time: 76.3 us; the launch traced here: 76 us
  blocking collectives  57 us (75%)
  Pallas kernels  8.85 us (12%)
  starting transfers between devices  6.86 us (9%)
  waiting for transfers between devices  1.7 us (2%)
  local copies, waits for them, and re-layouts  0.93 us (1%)
    all_to_all x1, blocking collectives, body(): lax.all_to_all(send.reshape(PARTS, FIVE, 2, LANES), 'azim', 0, 0, tiled=T...  29 us
    all_to_all x1, blocking collectives, body(): lax.all_to_all(spectrum.reshape(PARTS, FIVE, 2, LANES), 'azim', 0, 0, til...  16.6 us
    all_to_all x1, blocking collectives, body(): lax.all_to_all(jnp.broadcast_to(owned[None], (4, 640, LANES)), 'tm', 0, 0...  11.4 us
    ppermute x1, starting transfers between devices, body(): theirs = lax.ppermute(mine, 'tm', [(i, i ^ 1) for i in range(8)])  6.86 us
    pallas_call x1, Pallas kernels, body(): pl.pallas_call(gram_kernel, grid_spec=pltpu.PrefetchScalarGridSpec(num_sc...  5.06 us
    pallas_call x1, Pallas kernels, body(): pl.pallas_call(transform_kernel, out_shape=jax.ShapeDtypeStruct((640, LAN...  2.08 us
    pallas_call x1, Pallas kernels, body(): pl.pallas_call(spread_kernel, out_shape=jax.ShapeDtypeStruct((640, LANES)...  1.71 us
    ppermute x1, waiting for transfers between devices, body(): theirs = lax.ppermute(mine, 'tm', [(i, i ^ 1) for i in range(8)])  1.7 us
  transfers between devices with their start and end apart: 1, of which 1 were waited for; matrix products, arithmetic and copies ran while one was open for 0% of the time, Pallas kernels for 0%

profile of v1, /device:TPU:1, one launch (start us, length us, event | category | flops | bytes accessed | tf_op | source)
XLA Modules:
  0.0 76.0 jit_solution(1589293960004848737)
XLA Ops:
  0.6 1.7 %spread.1 = bf16[640,128]{1,0:T(8,128)(2,1)} custom-call(bf16[4,160,128]{2,1,0:T(8,128)(2,1)} %x_ref.1), custom_call_target="tpu_custom_call" | custom-call | tf_op jit(solution)/shard_map/spread/pallas_call | solution.py:95
  2.3 29.0 %all_to_all.15 = bf16[64,5,2,128]{3,2,1,0:T(2,128)(2,1)} all-to-all(bf16[64,5,2,128]{3,2,1,0:T(2,128)(2,1)} %bitcast.7), channel_id=1, replica_groups=mesh['tm'=8,'azim'=64] {'azim'}, dimensions={0} | all-to-all | bytes 327680 | tf_op jit(solution)/shard_map/all_to_all | solution.py:101
  31.3 2.1 %transform.1 = bf16[640,128]{1,0:T(8,128)(2,1)} custom-call(bf16[640,128]{1,0:T(8,128)(2,1)} %bitcast.5, bf16[512,128]{1,0:T(8,128)(2,1)} %constant.8.clone.t_ref), custom_call_target="tpu_custom_call" | custom-call | tf_op jit(solution)/shard_map/transform/pallas_call | solution.py:102
  33.4 16.6 %all_to_all.16 = bf16[64,5,2,128]{3,2,1,0:T(2,128)(2,1)S(1)} all-to-all(bf16[64,5,2,128]{3,2,1,0:T(2,128)(2,1)} %bitcast.6), channel_id=1, replica_groups=mesh['tm'=8,'azim'=64] {'azim'}, dimensions={0} | all-to-all | bytes 327680 | tf_op jit(solution)/shard_map/all_to_all | solution.py:108
  50.0 0.1 broadcast_in_dim.8
  50.1 11.4 %all_to_all.17.a_ref = bf16[4,640,128]{2,1,0:T(8,128)(2,1)S(1)} all-to-all(bf16[4,640,128]{2,1,0:T(8,128)(2,1)S(1)} %broadcast_in_dim.8), channel_id=1, replica_groups={{0,128,256,384},{64,192,320,448},{1,129,257,385},{65,193,321,449},{2,13..., dimensions={0} | all-to-all | bytes 1310720 | tf_op jit(solution)/shard_map/all_to_all | solution.py:111
  61.5 0.0 copy-start
  61.5 6.9 %collective-permute-start = (bf16[4,640,128]{2,1,0:T(8,128)(2,1)S(1)}, bf16[4,640,128]{2,1,0:T(8,128)(2,1)S(1)}, u32[]{:S(2)}, u32[]{:S(2)}) collective-permute-start(bf16[4,640,128]{2,1,0:T(8,128)(2,1)S(1)} %all_to_all.17.a_ref), channel_id=1, source_target_pairs={{0,64},{64,0},{128,192},{192,128},{256,320},{320,256},{384,448},{4... | collective-permute-start | bytes 1966088 | tf_op jit(solution)/shard_map/ppermute | solution.py:114
  68.4 1.7 %collective-permute-done.b_ref = bf16[4,640,128]{2,1,0:T(8,128)(2,1)S(1)} collective-permute-done((bf16[4,640,128]{2,1,0:T(8,128)(2,1)S(1)}, bf16[4,640,128]{2,1,0:T(8,128)(2,1)S(1)}, u32[]{:S(2)}, u32[]{:S(2)}) %collective-permute-start) | collective-permute-done | bytes 655392 | tf_op jit(solution)/shard_map/ppermute | solution.py:114
  70.1 0.0 copy-start.1
  70.1 0.0 copy-done
  70.1 0.8 %copy-done.1 = bf16[4,640,128]{2,1,0:T(8,128)(2,1)} copy-done((bf16[4,640,128]{2,1,0:T(8,128)(2,1)}, bf16[4,640,128]{2,1,0:T(8,128)(2,1)S(1)}, u32[]{:S(2)}) %copy-start.1) | copy-done | bytes 655384
  70.9 5.1 %gram.1 = (f32[2,2,128,1024]{3,2,1,0:T(8,128)}, f32[2,2,128,1024]{3,2,1,0:T(8,128)}) custom-call(s32[1]{0:T(128)} %bitcast.idx_ref, bf16[4,640,128]{2,1,0:T(8,128)(2,1)} %copy-done, bf16[4,640,128]{2,1,0:T(8,128)(2,1)} %copy-done.1), custom_call_target="tpu_custom_call" | custom-call | tf_op jit(solution)/shard_map/gram/pallas_call | solution.py:118
Async XLA Ops:
  61.5 8.6 %copy-start = (bf16[4,640,128]{2,1,0:T(8,128)(2,1)}, bf16[4,640,128]{2,1,0:T(8,128)(2,1)S(1)}, u32[]{:S(2)}) copy-start(bf16[4,640,128]{2,1,0:T(8,128)(2,1)S(1)} %all_to_all.17.a_ref) | copy-start | bytes 1966084
  61.5 8.6 %collective-permute-start = (bf16[4,640,128]{2,1,0:T(8,128)(2,1)S(1)}, bf16[4,640,128]{2,1,0:T(8,128)(2,1)S(1)}, u32[]{:S(2)}, u32[]{:S(2)}) collective-permute-start(bf16[4,640,128]{2,1,0:T(8,128)(2,1)S(1)} %all_to_all.17.a_ref), channel_id=1, source_target_pairs={{0,64},{64,0},{128,192},{192,128},{256,320},{320,256},{384,448},{4... | collective-permute-start | bytes 1966088 | tf_op jit(solution)/shard_map/ppermute | solution.py:114
  70.1 0.8 %copy-start.1 = (bf16[4,640,128]{2,1,0:T(8,128)(2,1)}, bf16[4,640,128]{2,1,0:T(8,128)(2,1)S(1)}, u32[]{:S(2)}) copy-start(bf16[4,640,128]{2,1,0:T(8,128)(2,1)S(1)} %collective-permute-done.b_ref) | copy-start | bytes 1966084

commit v2 on v1

v2 whole, which is shorter than its diff:
```python
import jax
import jax.numpy as jnp
import numpy as np
from jax import lax
from jax.experimental import pallas as pl
from jax.experimental.pallas import tpu as pltpu
from jax.sharding import PartitionSpec as P

THETA = 256
MODES = 128
ROWS = 160
LANES = 128
HALF = 64
PARTS = 64
FIVE = 5
CELL = 2 * FIVE


def make_table():
    b, alo, p, k, ahi, s = np.meshgrid(
        np.arange(2), np.arange(2), np.arange(2), np.arange(64), np.arange(2), np.arange(64), indexing="ij"
    )
    angle = 4 * s + 2 * ahi + alo
    wave = 2 * k + b
    phase = ((angle * wave) % THETA).astype(np.float32) * np.float32(2.0 * np.pi / THETA)
    values = np.where(p == 1, -np.sin(phase), np.cos(phase)) * np.float32(THETA ** (-0.5))
    return values.astype(np.float32).reshape(512, 128).astype(jnp.bfloat16)


def low_lanes(shape):
    return lax.broadcasted_iota(jnp.int32, shape, 1) < HALF


def spread_kernel(x_ref, o_ref, scr):
    low = low_lanes((ROWS, LANES))
    for ahi in range(2):
        even = x_ref[2 * ahi].astype(jnp.float32)
        odd = x_ref[2 * ahi + 1].astype(jnp.float32)
        scr[pl.ds(ahi, ROWS, stride=2), :] = jnp.where(low, even, pltpu.roll(odd, HALF, 1))
        scr[pl.ds(2 * ROWS + ahi, ROWS, stride=2), :] = jnp.where(low, pltpu.roll(even, HALF, 1), odd)
    o_ref[...] = scr[...].astype(jnp.bfloat16)


def transform_kernel(x_ref, t_ref, o_ref, scr_in, scr_out):
    half = lax.axis_index("azim") // (PARTS // 2)
    one = t_ref[pl.ds(pl.multiple_of(256 * half, 256), 256)]
    two = t_ref[pl.ds(pl.multiple_of(256 * (1 - half), 256), 256)]
    scr_in[...] = x_ref[...].astype(jnp.float32)
    low = low_lanes((LANES, LANES))
    for r5 in range(FIVE):
        field = jnp.concatenate(
            [scr_in[pl.ds(2 * r5 + ahi, PARTS, stride=CELL), :] for ahi in range(2)], axis=0
        ).astype(jnp.bfloat16)
        y = jnp.dot(one, field, preferred_element_type=jnp.float32)
        w = jnp.dot(two, field, preferred_element_type=jnp.float32)
        straight = jnp.where(low, y[0:128], w[128:256])
        crossed = jnp.where(low, w[0:128], y[128:256])
        both = straight + pltpu.roll(crossed, HALF, 1)
        for p in range(2):
            scr_out[pl.ds(2 * r5 + p, PARTS, stride=CELL), :] = both[64 * p : 64 * p + 64]
    o_ref[...] = scr_out[...].astype(jnp.bfloat16)


def gram_kernel(idx_ref, a_ref, b_ref, xx_ref, xy_ref, right, left):
    m = pl.program_id(0)
    tm = idx_ref[0]
    core = lax.rem(tm, 2)

    @pl.when(m == 0)
    def _():
        low = low_lanes((2 * ROWS, LANES))
        for own, ref in ((True, a_ref), (False, b_ref)):
            par = core if own else 1 - core
            for x in range(4):
                first = ref[x, 0 : 2 * ROWS]
                second = ref[x, 2 * ROWS : 4 * ROWS]
                at = pl.multiple_of((2 * x + par) * LANES, LANES)
                right[0, :, pl.ds(at, LANES)] = jnp.where(low, first, second)
                right[1, :, pl.ds(at, LANES)] = pltpu.roll(jnp.where(low, second, first), HALF, 1)
        even = lax.rem(lax.broadcasted_iota(jnp.int32, (2 * ROWS, LANES), 0), 2) == 0
        here = pl.multiple_of(tm * LANES, LANES)
        for n in range(2):
            f = right[n, :, pl.ds(here, LANES)].astype(jnp.float32)
            turned = jnp.where(even, -pltpu.roll(f, 2 * ROWS - 1, 0), pltpu.roll(f, 1, 0))
            left[n, :LANES] = f.T.astype(jnp.bfloat16)
            left[n, LANES:] = turned.T.astype(jnp.bfloat16)

    g = jnp.dot(left[m], right[m], preferred_element_type=jnp.float32) * jnp.float32(ROWS ** (-0.5))
    col = lax.broadcasted_iota(jnp.int32, g.shape, 1)
    keep = col < (tm + 1) * LANES
    xx = jnp.where(keep, g, 0.0)
    xy = jnp.where(keep & (col < g.shape[1] - 1), pltpu.roll(g, g.shape[1] - 1, 1), 0.0)
    for p in range(2):
        xx_ref[0, p] = xx[p * LANES : (p + 1) * LANES]
        xy_ref[0, p] = xy[p * LANES : (p + 1) * LANES]


def near(array):
    return pltpu.with_memory_space_constraint(array, pltpu.VMEM)


def body(pressure):
    f32 = jnp.float32
    bf16 = jnp.bfloat16
    tm = lax.axis_index("tm")
    vmem = pl.BlockSpec(memory_space=pltpu.VMEM)
    send = pl.pallas_call(
        spread_kernel,
        out_shape=pltpu.VMEM((640, LANES), bf16),
        in_specs=[vmem],
        out_specs=vmem,
        scratch_shapes=[pltpu.VMEM((640, LANES), f32)],
        name="spread",
    )(pressure)
    got = lax.all_to_all(send.reshape(PARTS, FIVE, 2, LANES), "azim", 0, 0, tiled=True)
    spectrum = pl.pallas_call(
        transform_kernel,
        out_shape=pltpu.VMEM((640, LANES), bf16),
        in_specs=[vmem, vmem],
        out_specs=vmem,
        scratch_shapes=[pltpu.VMEM((640, LANES), f32), pltpu.VMEM((640, LANES), f32)],
        name="transform",
    )(near(got.reshape(640, LANES)), near(jnp.asarray(make_table())))
    owned = lax.all_to_all(spectrum.reshape(PARTS, FIVE, 2, LANES), "azim", 0, 0, tiled=True)
    owned = owned.reshape(640, LANES)
    chips = [[2 * x + c for x in range(4)] for c in range(2)]
    mine = lax.all_to_all(
        jnp.broadcast_to(owned[None], (4, 640, LANES)), "tm", 0, 0, tiled=True, axis_index_groups=chips
    )
    theirs = lax.ppermute(mine, "tm", [(i, i ^ 1) for i in range(8)])
    out = jax.ShapeDtypeStruct((2, 2, LANES, 1024), f32)
    block = pl.BlockSpec((1, 2, LANES, 1024), lambda i, idx: (i, 0, 0, 0))
    return pl.pallas_call(
        gram_kernel,
        grid_spec=pltpu.PrefetchScalarGridSpec(
            num_scalar_prefetch=1,
            grid=(2,),
            in_specs=[vmem, vmem],
            out_specs=[block, block],
            scratch_shapes=[pltpu.VMEM((2, 2 * ROWS, 1024), bf16), pltpu.VMEM((2, 2 * LANES, 2 * ROWS), bf16)],
        ),
        out_shape=(out, out),
        name="gram",
    )(tm.astype(jnp.int32).reshape(1), near(mine), near(theirs))


def solution(mesh):
    in_specs = (P("azim", None, "tm"),)
    out_specs = (P("azim", None, "tm", None), P("azim", None, "tm", None))
    return jax.shard_map(body, mesh=mesh, in_specs=in_specs, out_specs=out_specs, check_vma=False)
```

time: 76.3 us -> 70.7 us (0.927)
  Pallas kernels: 8.85 us -> 4.45 us
    pallas_call x2, Pallas kernels: 3.79 us -> 1.46 us  [the longest x1 1.04 us: body(): pl.pallas_call(spread_kernel, out_shape=pltpu.VMEM((640, LANES), bf16), i...]
    pallas_call x1, Pallas kernels: 5.06 us -> 2.98 us  [body(): pl.pallas_call(gram_kernel, grid_spec=pltpu.PrefetchScalarGridSpec(num_sc...]
where the time goes in v2:
time: 70.7 us; the launch traced here: 70.4 us
  blocking collectives  56.3 us (80%)
  starting transfers between devices  6.28 us (9%)
  Pallas kernels  4.45 us (6%)
  waiting for transfers between devices  1.7 us (2%)
  local copies, waits for them, and re-layouts  0.99 us (1%)
    all_to_all x1, blocking collectives, body(): lax.all_to_all(send.reshape(PARTS, FIVE, 2, LANES), 'azim', 0, 0, tiled=T...  28.7 us
    all_to_all x1, blocking collectives, body(): lax.all_to_all(spectrum.reshape(PARTS, FIVE, 2, LANES), 'azim', 0, 0, til...  16.2 us
    all_to_all x1, blocking collectives, body(): lax.all_to_all(jnp.broadcast_to(owned[None], (4, 640, LANES)), 'tm', 0, 0...  11.5 us
    ppermute x1, starting transfers between devices, body(): theirs = lax.ppermute(mine, 'tm', [(i, i ^ 1) for i in range(8)])  6.28 us
    pallas_call x1, Pallas kernels, body(): pl.pallas_call(gram_kernel, grid_spec=pltpu.PrefetchScalarGridSpec(num_sc...  2.98 us
    ppermute x1, waiting for transfers between devices, body(): theirs = lax.ppermute(mine, 'tm', [(i, i ^ 1) for i in range(8)])  1.7 us
  transfers between devices with their start and end apart: 1, of which 1 were waited for; matrix products, arithmetic and copies ran while one was open for 0% of the time, Pallas kernels for 0%

profile of v2, /device:TPU:1, one launch (start us, length us, event | category | flops | bytes accessed | tf_op | source)
XLA Modules:
  0.0 70.4 jit_solution(10717917610893878774)
XLA Ops:
  0.6 1.0 %spread.1 = bf16[640,128]{1,0:T(8,128)(2,1)S(1)} custom-call(bf16[4,160,128]{2,1,0:T(8,128)(2,1)} %x_ref.1), custom_call_target="tpu_custom_call" | custom-call | tf_op jit(solution)/shard_map/spread/pallas_call | solution.py:107
  1.7 28.7 %all_to_all.15 = bf16[64,5,2,128]{3,2,1,0:T(2,128)(2,1)S(1)} all-to-all(bf16[64,5,2,128]{3,2,1,0:T(2,128)(2,1)S(1)} %bitcast.7), channel_id=1, replica_groups=mesh['tm'=8,'azim'=64] {'azim'}, dimensions={0} | all-to-all | bytes 327680 | tf_op jit(solution)/shard_map/all_to_all | solution.py:115
  30.4 0.0 copy-start
  30.4 0.9 %copy-done = bf16[512,128]{1,0:T(8,128)(2,1)S(1)} copy-done((bf16[512,128]{1,0:T(8,128)(2,1)S(1)}, bf16[512,128]{1,0:T(8,128)(2,1)}, u32[]{:S(2)}) %copy-start) | copy-done | bytes 131096
  31.3 0.4 transform.1
  31.7 16.2 %all_to_all.16 = bf16[64,5,2,128]{3,2,1,0:T(2,128)(2,1)S(1)} all-to-all(bf16[64,5,2,128]{3,2,1,0:T(2,128)(2,1)S(1)} %bitcast.6), channel_id=1, replica_groups=mesh['tm'=8,'azim'=64] {'azim'}, dimensions={0} | all-to-all | bytes 327680 | tf_op jit(solution)/shard_map/all_to_all | solution.py:124
  47.9 0.1 broadcast_in_dim.8
  48.0 11.5 %all_to_all.17.a_ref = bf16[4,640,128]{2,1,0:T(8,128)(2,1)S(1)} all-to-all(bf16[4,640,128]{2,1,0:T(8,128)(2,1)S(1)} %broadcast_in_dim.8), channel_id=1, replica_groups={{0,128,256,384},{64,192,320,448},{1,129,257,385},{65,193,321,449},{2,13..., dimensions={0} | all-to-all | bytes 1310720 | tf_op jit(solution)/shard_map/all_to_all | solution.py:127
  59.5 6.3 %collective-permute-start = (bf16[4,640,128]{2,1,0:T(8,128)(2,1)S(1)}, bf16[4,640,128]{2,1,0:T(8,128)(2,1)S(1)}, u32[]{:S(2)}, u32[]{:S(2)}) collective-permute-start(bf16[4,640,128]{2,1,0:T(8,128)(2,1)S(1)} %all_to_all.17.a_ref), channel_id=1, source_target_pairs={{0,64},{64,0},{128,192},{192,128},{256,320},{320,256},{384,448},{4... | collective-permute-start | bytes 1966088 | tf_op jit(solution)/shard_map/ppermute | solution.py:130
  65.7 1.7 %collective-permute-done.b_ref = bf16[4,640,128]{2,1,0:T(8,128)(2,1)S(1)} collective-permute-done((bf16[4,640,128]{2,1,0:T(8,128)(2,1)S(1)}, bf16[4,640,128]{2,1,0:T(8,128)(2,1)S(1)}, u32[]{:S(2)}, u32[]{:S(2)}) %collective-permute-start) | collective-permute-done | bytes 655392 | tf_op jit(solution)/shard_map/ppermute | solution.py:130
  67.4 3.0 %gram.1 = (f32[2,2,128,1024]{3,2,1,0:T(8,128)}, f32[2,2,128,1024]{3,2,1,0:T(8,128)}) custom-call(s32[1]{0:T(128)} %bitcast.idx_ref, bf16[4,640,128]{2,1,0:T(8,128)(2,1)S(1)} %all_to_all.17.a_ref, bf16[4,640,128]{2,1,0:T(8,128)(2,1)S(1)} %collective-permute-done.b_ref), custom_call_target="tpu_custom_call" | custom-call | tf_op jit(solution)/shard_map/gram/pallas_call | solution.py:133
Async XLA Ops:
  30.4 0.9 %copy-start = (bf16[512,128]{1,0:T(8,128)(2,1)S(1)}, bf16[512,128]{1,0:T(8,128)(2,1)}, u32[]{:S(2)}) copy-start(bf16[512,128]{1,0:T(8,128)(2,1)} %constant.8.clone.t_ref) | copy-start | bytes 393220
  59.5 8.0 %collective-permute-start = (bf16[4,640,128]{2,1,0:T(8,128)(2,1)S(1)}, bf16[4,640,128]{2,1,0:T(8,128)(2,1)S(1)}, u32[]{:S(2)}, u32[]{:S(2)}) collective-permute-start(bf16[4,640,128]{2,1,0:T(8,128)(2,1)S(1)} %all_to_all.17.a_ref), channel_id=1, source_target_pairs={{0,64},{64,0},{128,192},{192,128},{256,320},{320,256},{384,448},{4... | collective-permute-start | bytes 1966088 | tf_op jit(solution)/shard_map/ppermute | solution.py:130

commit v3 on v2

v3 whole, which is shorter than its diff:
```python
import jax
import jax.numpy as jnp
import numpy as np
from jax import lax
from jax.experimental import pallas as pl
from jax.experimental.pallas import tpu as pltpu
from jax.sharding import PartitionSpec as P

THETA = 256
MODES = 128
ROWS = 160
LANES = 128
HALF = 64
PARTS = 64
FIVE = 5
CELL = 2 * FIVE


def make_table():
    b, alo, p, k, ahi, s = np.meshgrid(
        np.arange(2), np.arange(2), np.arange(2), np.arange(64), np.arange(2), np.arange(64), indexing="ij"
    )
    angle = 4 * s + 2 * ahi + alo
    wave = 2 * k + b
    phase = ((angle * wave) % THETA).astype(np.float32) * np.float32(2.0 * np.pi / THETA)
    values = np.where(p == 1, -np.sin(phase), np.cos(phase)) * np.float32(THETA ** (-0.5))
    return values.astype(np.float32).reshape(512, 128).astype(jnp.bfloat16)


def low_lanes(shape):
    return lax.broadcasted_iota(jnp.int32, shape, 1) < HALF


def spread_kernel(x_ref, t_ref, o_ref, table_ref, near_ref, scr, sems):
    fetch = [
        pltpu.make_async_copy(x_ref.at[pl.ds(2 * ahi, 2)], near_ref.at[pl.ds(2 * ahi, 2)], sems.at[ahi])
        for ahi in range(2)
    ]
    fetch.append(pltpu.make_async_copy(t_ref, table_ref, sems.at[2]))
    for copy in fetch:
        copy.start()
    low = low_lanes((ROWS, LANES))
    for ahi in range(2):
        fetch[ahi].wait()
        even = near_ref[2 * ahi].astype(jnp.float32)
        odd = near_ref[2 * ahi + 1].astype(jnp.float32)
        scr[pl.ds(ahi, ROWS, stride=2), :] = jnp.where(low, even, pltpu.roll(odd, HALF, 1))
        scr[pl.ds(2 * ROWS + ahi, ROWS, stride=2), :] = jnp.where(low, pltpu.roll(even, HALF, 1), odd)
    o_ref[...] = scr[...].astype(jnp.bfloat16)
    fetch[2].wait()


def transform_kernel(x_ref, t_ref, o_ref, scr_in, scr_out):
    half = lax.axis_index("azim") // (PARTS // 2)
    one = t_ref[pl.ds(pl.multiple_of(256 * half, 256), 256)]
    two = t_ref[pl.ds(pl.multiple_of(256 * (1 - half), 256), 256)]
    scr_in[...] = x_ref[...].astype(jnp.float32)
    low = low_lanes((LANES, LANES))
    for r5 in range(FIVE):
        field = jnp.concatenate(
            [scr_in[pl.ds(2 * r5 + ahi, PARTS, stride=CELL), :] for ahi in range(2)], axis=0
        ).astype(jnp.bfloat16)
        y = jnp.dot(one, field, preferred_element_type=jnp.float32)
        w = jnp.dot(two, field, preferred_element_type=jnp.float32)
        straight = jnp.where(low, y[0:128], w[128:256])
        crossed = jnp.where(low, w[0:128], y[128:256])
        both = straight + pltpu.roll(crossed, HALF, 1)
        for p in range(2):
            scr_out[pl.ds(2 * r5 + p, PARTS, stride=CELL), :] = both[64 * p : 64 * p + 64]
    o_ref[...] = scr_out[...].astype(jnp.bfloat16)


GAIN = ROWS ** (-0.5)
CHIPS = 4
WIDE = CHIPS * LANES
GRANT = pltpu.CompilerParams(vmem_limit_bytes=16 << 20)


def mode_rows(ref, x, m):
    low = low_lanes((2 * ROWS, LANES))
    first = ref[x, 0 : 2 * ROWS]
    second = ref[x, 2 * ROWS : 4 * ROWS]
    if m == 0:
        return jnp.where(low, first, second)
    return pltpu.roll(jnp.where(low, second, first), HALF, 1)


def wide_rows(ref, m):
    return jnp.concatenate([mode_rows(ref, x, m) for x in range(CHIPS)], axis=1)


def tile_copy(src, dst, m, x, par, sem):
    at = pl.multiple_of((2 * x + par) * LANES, LANES)
    return pltpu.make_async_copy(src.at[m, x], dst.at[m, :, :, pl.ds(at, LANES)], sem)


def store_tile(ref, m, x, value):
    ref[m, x, 0] = value[:LANES]
    ref[m, x, 1] = value[LANES:]


def own_kernel(mine_ref, xx_ref, left_ref, next_ref, tile, sems):
    tm = lax.axis_index("tm")
    core = lax.rem(tm, 2)
    even = lax.rem(lax.broadcasted_iota(jnp.int32, (2 * ROWS, LANES), 0), 2) == 0
    for m in range(2):
        f = mode_rows(mine_ref, lax.div(tm, 2), m).astype(jnp.float32)
        turned = jnp.where(even, -pltpu.roll(f, 2 * ROWS - 1, 0), pltpu.roll(f, 1, 0))
        left_ref[m, :LANES] = f.T.astype(jnp.bfloat16)
        left_ref[m, LANES:] = turned.T.astype(jnp.bfloat16)
        g = jnp.dot(left_ref[m], wide_rows(mine_ref, m), preferred_element_type=jnp.float32) * jnp.float32(GAIN)
        for x in range(CHIPS):
            block = g[:, x * LANES : (x + 1) * LANES]
            store_tile(tile, m, x, jnp.where(2 * x + core <= tm, block, 0.0))
            tile_copy(tile, xx_ref, m, x, core, sems.at[m, x]).start()
            next_ref[m, x] = pltpu.roll(block, LANES - 1, 1)
        next_ref[m, CHIPS] = jnp.zeros((2 * LANES, LANES), jnp.float32)
    for m in range(2):
        for x in range(CHIPS):
            tile_copy(tile, xx_ref, m, x, core, sems.at[m, x]).wait()


def partner_kernel(theirs_ref, left_ref, next_ref, old_ref, xx_ref, xy_ref, tile, pair, ynext, sems, ysems):
    del old_ref
    tm = lax.axis_index("tm")
    core = lax.rem(tm, 2)
    other = 1 - core
    inner = lax.broadcasted_iota(jnp.int32, (2 * LANES, LANES), 1) < LANES - 1
    for m in range(2):
        g = jnp.dot(left_ref[m], wide_rows(theirs_ref, m), preferred_element_type=jnp.float32) * jnp.float32(GAIN)
        for x in range(CHIPS):
            block = g[:, x * LANES : (x + 1) * LANES]
            keep = 2 * x + other <= tm
            store_tile(tile, m, x, jnp.where(keep, block, 0.0))
            tile_copy(tile, xx_ref, m, x, other, sems.at[m, x]).start()
            shifted = pltpu.roll(block, LANES - 1, 1)
            ynext[m, x] = shifted
            whole = jnp.where(inner, shifted, next_ref[m, x + 1 - core])
            store_tile(pair.at[1], m, x, jnp.where(keep, whole, 0.0))
            tile_copy(pair.at[1], xy_ref, m, x, other, ysems.at[1, m, x]).start()
        ynext[m, CHIPS] = jnp.zeros((2 * LANES, LANES), jnp.float32)
        for x in range(CHIPS):
            whole = jnp.where(inner, next_ref[m, x], ynext[m, x + core])
            store_tile(pair.at[0], m, x, jnp.where(2 * x + core <= tm, whole, 0.0))
            tile_copy(pair.at[0], xy_ref, m, x, core, ysems.at[0, m, x]).start()
    for m in range(2):
        for x in range(CHIPS):
            tile_copy(tile, xx_ref, m, x, other, sems.at[m, x]).wait()
            tile_copy(pair.at[1], xy_ref, m, x, other, ysems.at[1, m, x]).wait()
            tile_copy(pair.at[0], xy_ref, m, x, core, ysems.at[0, m, x]).wait()


def near(array):
    return pltpu.with_memory_space_constraint(array, pltpu.VMEM)


def kept(array):
    return pltpu.with_memory_space_constraint(array, pltpu.HBM)


def body(pressure):
    f32 = jnp.float32
    bf16 = jnp.bfloat16
    vmem = pl.BlockSpec(memory_space=pltpu.VMEM)
    hbm = pl.BlockSpec(memory_space=pl.ANY)
    far = pl.BlockSpec(memory_space=pltpu.HBM)
    table = jnp.asarray(make_table())
    send, table = pl.pallas_call(
        spread_kernel,
        out_shape=(pltpu.VMEM((640, LANES), bf16), pltpu.VMEM(table.shape, bf16)),
        in_specs=[far, far],
        out_specs=(vmem, vmem),
        scratch_shapes=[
            pltpu.VMEM(pressure.shape, bf16),
            pltpu.VMEM((640, LANES), f32),
            pltpu.SemaphoreType.DMA((3,)),
        ],
        compiler_params=GRANT,
        name="spread",
    )(kept(pressure), kept(table))
    got = lax.all_to_all(send.reshape(PARTS, FIVE, 2, LANES), "azim", 0, 0, tiled=True)
    spectrum = pl.pallas_call(
        transform_kernel,
        out_shape=pltpu.VMEM((640, LANES), bf16),
        in_specs=[vmem, vmem],
        out_specs=vmem,
        scratch_shapes=[pltpu.VMEM((640, LANES), f32), pltpu.VMEM((640, LANES), f32)],
        compiler_params=GRANT,
        name="transform",
    )(near(got.reshape(640, LANES)), near(table))
    owned = lax.all_to_all(spectrum.reshape(PARTS, FIVE, 2, LANES), "azim", 0, 0, tiled=True)
    owned = owned.reshape(640, LANES)
    chips = [[2 * x + c for x in range(CHIPS)] for c in range(2)]
    mine = lax.all_to_all(
        jnp.broadcast_to(owned[None], (CHIPS, 640, LANES)), "tm", 0, 0, tiled=True, axis_index_groups=chips
    )
    theirs = lax.ppermute(mine, "tm", [(i, i ^ 1) for i in range(2 * CHIPS)])
    out = jax.ShapeDtypeStruct((2, 2, LANES, 2 * WIDE), f32)
    tile = pltpu.VMEM((2, CHIPS, 2, LANES, LANES), f32)
    steps = (2, CHIPS + 1, 2 * LANES, LANES)
    gram_xx, left, after = pl.pallas_call(
        own_kernel,
        out_shape=(out, pltpu.VMEM((2, 2 * LANES, 2 * ROWS), bf16), pltpu.VMEM(steps, f32)),
        in_specs=[vmem],
        out_specs=(hbm, vmem, vmem),
        scratch_shapes=[tile, pltpu.SemaphoreType.DMA((2, CHIPS))],
        compiler_params=GRANT,
        name="own",
    )(near(mine))
    return pl.pallas_call(
        partner_kernel,
        out_shape=(out, out),
        in_specs=[vmem, vmem, vmem, hbm],
        out_specs=(hbm, hbm),
        scratch_shapes=[
            tile,
            pltpu.VMEM((2, 2, CHIPS, 2, LANES, LANES), f32),
            pltpu.VMEM(steps, f32),
            pltpu.SemaphoreType.DMA((2, CHIPS)),
            pltpu.SemaphoreType.DMA((2, 2, CHIPS)),
        ],
        input_output_aliases={3: 0},
        compiler_params=GRANT,
        name="partner",
    )(near(theirs), near(left), near(after), gram_xx)


def solution(mesh):
    in_specs = (P("azim", None, "tm"),)
    out_specs = (P("azim", None, "tm", None), P("azim", None, "tm", None))
    return jax.shard_map(body, mesh=mesh, in_specs=in_specs, out_specs=out_specs, check_vma=False)
```

time: 70.7 us -> 69.3 us (0.980)
  waiting for transfers between devices: 1.7 us -> 0.01 us
  Pallas kernels: 4.45 us -> 5.62 us
  local copies, waits for them, and re-layouts: 0.99 us -> 0.09 us
    ppermute x1, waiting for transfers between devices: 1.7 us -> 0.01 us  [body(): theirs = lax.ppermute(mine, 'tm', [(i, i ^ 1) for i in range(2 * CHIPS)])]
    pallas_call x2 -> x3, Pallas kernels: 4.03 us -> 5.2 us  [the longest x1 2.32 us: body(): pl.pallas_call(partner_kernel, out_shape=(out, out), in_specs=[vmem, vmem...]
    unnamed x2 -> x0, local copies, waits for them, and re-layouts: 0.9 us -> none
  transfers between devices with their start and end apart: 1 -> 1, of which waited for: 1 -> 0; matrix products, arithmetic and copies ran while one was open for 0% -> 0% of each run, Pallas kernels for 0% -> 3%
where the time goes in v3:
time: 69.3 us; the launch traced here: 69 us
  blocking collectives  56.4 us (81%)
  starting transfers between devices  6.28 us (9%)
  Pallas kernels  5.62 us (8%)
    all_to_all x1, blocking collectives, body(): lax.all_to_all(send.reshape(PARTS, FIVE, 2, LANES), 'azim', 0, 0, tiled=T...  28.7 us
    all_to_all x1, blocking collectives, body(): lax.all_to_all(spectrum.reshape(PARTS, FIVE, 2, LANES), 'azim', 0, 0, til...  16.2 us
    all_to_all x1, blocking collectives, body(): lax.all_to_all(jnp.broadcast_to(owned[None], (CHIPS, 640, LANES)), 'tm',...  11.5 us
    ppermute x1, starting transfers between devices, body(): theirs = lax.ppermute(mine, 'tm', [(i, i ^ 1) for i in range(2 * CHIPS)])  6.28 us
    pallas_call x1, Pallas kernels, body(): pl.pallas_call(partner_kernel, out_shape=(out, out), in_specs=[vmem, vmem...  2.32 us
    pallas_call x1, Pallas kernels, body(): pl.pallas_call(own_kernel, out_shape=(out, pltpu.VMEM((2, 2 * LANES, 2 *...  1.75 us
  transfers between devices with their start and end apart: 1, of which 0 were waited for; matrix products, arithmetic and copies ran while one was open for 0% of the time, Pallas kernels for 3%

profile of v3, /device:TPU:1, one launch (start us, length us, event | category | flops | bytes accessed | tf_op | source)
XLA Modules:
  0.0 69.0 jit_solution(759126901929630469)
XLA Ops:
  0.6 1.1 %spread.1 = (bf16[640,128]{1,0:T(8,128)(2,1)S(1)}, bf16[512,128]{1,0:T(8,128)(2,1)S(1)}) custom-call(bf16[4,160,128]{2,1,0:T(8,128)(2,1)} %x_ref.1, bf16[512,128]{1,0:T(8,128)(2,1)} %constant.2.clone.t_ref), custom_call_target="tpu_custom_call" | custom-call | tf_op jit(solution)/shard_map/spread/pallas_call | solution.py:168
  1.8 28.7 %all_to_all.15 = bf16[64,5,2,128]{3,2,1,0:T(2,128)(2,1)S(1)} all-to-all(bf16[64,5,2,128]{3,2,1,0:T(2,128)(2,1)S(1)} %bitcast.6), channel_id=1, replica_groups=mesh['tm'=8,'azim'=64] {'azim'}, dimensions={0} | all-to-all | bytes 327680 | tf_op jit(solution)/shard_map/all_to_all | solution.py:181
  30.4 0.4 transform.1
  30.9 16.2 %all_to_all.16 = bf16[64,5,2,128]{3,2,1,0:T(2,128)(2,1)S(1)} all-to-all(bf16[64,5,2,128]{3,2,1,0:T(2,128)(2,1)S(1)} %bitcast.5), channel_id=1, replica_groups=mesh['tm'=8,'azim'=64] {'azim'}, dimensions={0} | all-to-all | bytes 327680 | tf_op jit(solution)/shard_map/all_to_all | solution.py:191
  47.1 0.1 broadcast_in_dim.8
  47.2 11.5 %all_to_all.17.mine_ref = bf16[4,640,128]{2,1,0:T(8,128)(2,1)S(1)} all-to-all(bf16[4,640,128]{2,1,0:T(8,128)(2,1)S(1)} %broadcast_in_dim.8), channel_id=1, replica_groups={{0,128,256,384},{64,192,320,448},{1,129,257,385},{65,193,321,449},{2,13..., dimensions={0} | all-to-all | bytes 1310720 | tf_op jit(solution)/shard_map/all_to_all | solution.py:194
  58.6 6.3 %collective-permute-start = (bf16[4,640,128]{2,1,0:T(8,128)(2,1)S(1)}, bf16[4,640,128]{2,1,0:T(8,128)(2,1)S(1)}, u32[]{:S(2)}, u32[]{:S(2)}) collective-permute-start(bf16[4,640,128]{2,1,0:T(8,128)(2,1)S(1)} %all_to_all.17.mine_ref), channel_id=1, source_target_pairs={{0,64},{64,0},{128,192},{192,128},{256,320},{320,256},{384,448},{4... | collective-permute-start | bytes 1966088 | tf_op jit(solution)/shard_map/ppermute | solution.py:197
  64.9 1.8 %own.1 = (f32[2,2,128,1024]{3,2,1,0:T(8,128)}, bf16[2,256,320]{2,1,0:T(8,128)(2,1)S(1)}, f32[2,5,256,128]{3,2,1,0:T(8,128)S(1)}) custom-call(bf16[4,640,128]{2,1,0:T(8,128)(2,1)S(1)} %all_to_all.17.mine_ref), custom_call_target="tpu_custom_call" | custom-call | tf_op jit(solution)/shard_map/own/pallas_call | solution.py:201
  66.7 0.0 collective-permute-done.theirs_ref
  66.7 2.3 %partner.1 = (f32[2,2,128,1024]{3,2,1,0:T(8,128)}, f32[2,2,128,1024]{3,2,1,0:T(8,128)}) custom-call(bf16[4,640,128]{2,1,0:T(8,128)(2,1)S(1)} %collective-permute-done.theirs_ref, bf16[2,256,320]{2,1,0:T(8,128)(2,1)S(1)} %get-tuple-element.9.left_ref, f32[2,5,256,128]{3,2,1,0:T(8,128)S(1)} %get-tuple-element.10.next_ref, ...), custom_call_target="tpu_custom_call", output_to_operand_aliasing={{0}: (3, {})} | custom-call | tf_op jit(solution)/shard_map/partner/pallas_call | solution.py:210
Async XLA Ops:
  58.6 8.1 %collective-permute-start = (bf16[4,640,128]{2,1,0:T(8,128)(2,1)S(1)}, bf16[4,640,128]{2,1,0:T(8,128)(2,1)S(1)}, u32[]{:S(2)}, u32[]{:S(2)}) collective-permute-start(bf16[4,640,128]{2,1,0:T(8,128)(2,1)S(1)} %all_to_all.17.mine_ref), channel_id=1, source_target_pairs={{0,64},{64,0},{128,192},{192,128},{256,320},{320,256},{384,448},{4... | collective-permute-start | bytes 1966088 | tf_op jit(solution)/shard_map/ppermute | solution.py:197

commit v4 on v3

--- a/solution.py
+++ b/solution.py
@@ -76,17 +76,20 @@
 GRANT = pltpu.CompilerParams(vmem_limit_bytes=16 << 20)
 
 
-def mode_rows(ref, x, m):
+def arrange_kernel(x_ref, o_ref):
     low = low_lanes((2 * ROWS, LANES))
-    first = ref[x, 0 : 2 * ROWS]
-    second = ref[x, 2 * ROWS : 4 * ROWS]
-    if m == 0:
-        return jnp.where(low, first, second)
-    return pltpu.roll(jnp.where(low, second, first), HALF, 1)
-
-
-def wide_rows(ref, m):
-    return jnp.concatenate([mode_rows(ref, x, m) for x in range(CHIPS)], axis=1)
+    first = x_ref[0 : 2 * ROWS]
+    second = x_ref[2 * ROWS : 4 * ROWS]
+    o_ref[0] = jnp.where(low, first, second)
+    o_ref[1] = pltpu.roll(jnp.where(low, second, first), HALF, 1)
+
+
+def blocks_of(left_ref, ref, m):
+    for x in range(0, CHIPS, 2):
+        rows = jnp.concatenate([ref[x, m], ref[x + 1, m]], axis=1)
+        g = jnp.dot(left_ref[m], rows, preferred_element_type=jnp.float32) * jnp.float32(GAIN)
+        yield x, g[:, :LANES]
+        yield x + 1, g[:, LANES:]
 
 
 def tile_copy(src, dst, m, x, par, sem):
@@ -103,18 +106,19 @@
     tm = lax.axis_index("tm")
     core = lax.rem(tm, 2)
     even = lax.rem(lax.broadcasted_iota(jnp.int32, (2 * ROWS, LANES), 0), 2) == 0
-    for m in range(2):
-        f = mode_rows(mine_ref, lax.div(tm, 2), m).astype(jnp.float32)
+
+    @pl.loop(0, 2)
+    def _(m):
+        f = mine_ref[lax.div(tm, 2), m].astype(jnp.float32)
         turned = jnp.where(even, -pltpu.roll(f, 2 * ROWS - 1, 0), pltpu.roll(f, 1, 0))
         left_ref[m, :LANES] = f.T.astype(jnp.bfloat16)
         left_ref[m, LANES:] = turned.T.astype(jnp.bfloat16)
-        g = jnp.dot(left_ref[m], wide_rows(mine_ref, m), preferred_element_type=jnp.float32) * jnp.float32(GAIN)
-        for x in range(CHIPS):
-            block = g[:, x * LANES : (x + 1) * LANES]
+        for x, block in blocks_of(left_ref, mine_ref, m):
             store_tile(tile, m, x, jnp.where(2 * x + core <= tm, block, 0.0))
             tile_copy(tile, xx_ref, m, x, core, sems.at[m, x]).start()
             next_ref[m, x] = pltpu.roll(block, LANES - 1, 1)
         next_ref[m, CHIPS] = jnp.zeros((2 * LANES, LANES), jnp.float32)
+
     for m in range(2):
         for x in range(CHIPS):
             tile_copy(tile, xx_ref, m, x, core, sems.at[m, x]).wait()
@@ -126,10 +130,10 @@
     core = lax.rem(tm, 2)
     other = 1 - core
     inner = lax.broadcasted_iota(jnp.int32, (2 * LANES, LANES), 1) < LANES - 1
-    for m in range(2):
-        g = jnp.dot(left_ref[m], wide_rows(theirs_ref, m), preferred_element_type=jnp.float32) * jnp.float32(GAIN)
-        for x in range(CHIPS):
-            block = g[:, x * LANES : (x + 1) * LANES]
+
+    @pl.loop(0, 2)
+    def _(m):
+        for x, block in blocks_of(left_ref, theirs_ref, m):
             keep = 2 * x + other <= tm
             store_tile(tile, m, x, jnp.where(keep, block, 0.0))
             tile_copy(tile, xx_ref, m, x, other, sems.at[m, x]).start()
@@ -143,6 +147,7 @@
             whole = jnp.where(inner, next_ref[m, x], ynext[m, x + core])
             store_tile(pair.at[0], m, x, jnp.where(2 * x + core <= tm, whole, 0.0))
             tile_copy(pair.at[0], xy_ref, m, x, core, ysems.at[0, m, x]).start()
+
     for m in range(2):
         for x in range(CHIPS):
             tile_copy(tile, xx_ref, m, x, other, sems.at[m, x]).wait()
@@ -189,10 +194,17 @@
         name="transform",
     )(near(got.reshape(640, LANES)), near(table))
     owned = lax.all_to_all(spectrum.reshape(PARTS, FIVE, 2, LANES), "azim", 0, 0, tiled=True)
-    owned = owned.reshape(640, LANES)
+    owned = pl.pallas_call(
+        arrange_kernel,
+        out_shape=pltpu.VMEM((2, 2 * ROWS, LANES), bf16),
+        in_specs=[vmem],
+        out_specs=vmem,
+        compiler_params=GRANT,
+        name="arrange",
+    )(near(owned.reshape(640, LANES)))
     chips = [[2 * x + c for x in range(CHIPS)] for c in range(2)]
     mine = lax.all_to_all(
-        jnp.broadcast_to(owned[None], (CHIPS, 640, LANES)), "tm", 0, 0, tiled=True, axis_index_groups=chips
+        jnp.broadcast_to(owned[None], (CHIPS,) + owned.shape), "tm", 0, 0, tiled=True, axis_index_groups=chips
     )
     theirs = lax.ppermute(mine, "tm", [(i, i ^ 1) for i in range(2 * CHIPS)])
     out = jax.ShapeDtypeStruct((2, 2, LANES, 2 * WIDE), f32)

time: 69.3 us -> 69.3 us (level)
  no operation moved by 1% of the time
where the time goes in v4:
time: 69.3 us; the launch traced here: 69.1 us
  blocking collectives  56.4 us (81%)
  starting transfers between devices  6.28 us (9%)
  Pallas kernels  5.65 us (8%)
    all_to_all x1, blocking collectives, body(): lax.all_to_all(send.reshape(PARTS, FIVE, 2, LANES), 'azim', 0, 0, tiled=T...  28.7 us
    all_to_all x1, blocking collectives, body(): lax.all_to_all(spectrum.reshape(PARTS, FIVE, 2, LANES), 'azim', 0, 0, til...  16.2 us
    all_to_all x1, blocking collectives, body(): lax.all_to_all(jnp.broadcast_to(owned[None], (CHIPS,) + owned.shape), 'tm...  11.5 us
    ppermute x1, starting transfers between devices, body(): theirs = lax.ppermute(mine, 'tm', [(i, i ^ 1) for i in range(2 * CHIPS)])  6.28 us
    pallas_call x1, Pallas kernels, body(): pl.pallas_call(partner_kernel, out_shape=(out, out), in_specs=[vmem, vmem...  2.23 us
    pallas_call x1, Pallas kernels, body(): pl.pallas_call(own_kernel, out_shape=(out, pltpu.VMEM((2, 2 * LANES, 2 *...  1.79 us
  transfers between devices with their start and end apart: 1, of which 0 were waited for; matrix products, arithmetic and copies ran while one was open for 0% of the time, Pallas kernels for 3%

profile of v4, /device:TPU:1, one launch (start us, length us, event | category | flops | bytes accessed | tf_op | source)
XLA Modules:
  0.0 69.1 jit_solution(16921457705347682171)
XLA Ops:
  0.6 1.1 %spread.1 = (bf16[640,128]{1,0:T(8,128)(2,1)S(1)}, bf16[512,128]{1,0:T(8,128)(2,1)S(1)}) custom-call(bf16[4,160,128]{2,1,0:T(8,128)(2,1)} %x_ref.1, bf16[512,128]{1,0:T(8,128)(2,1)} %constant.2.clone.t_ref), custom_call_target="tpu_custom_call" | custom-call | tf_op jit(solution)/shard_map/spread/pallas_call | solution.py:173
  1.8 28.7 %all_to_all.15 = bf16[64,5,2,128]{3,2,1,0:T(2,128)(2,1)S(1)} all-to-all(bf16[64,5,2,128]{3,2,1,0:T(2,128)(2,1)S(1)} %bitcast.7), channel_id=1, replica_groups=mesh['tm'=8,'azim'=64] {'azim'}, dimensions={0} | all-to-all | bytes 327680 | tf_op jit(solution)/shard_map/all_to_all | solution.py:186
  30.4 0.4 transform.1
  30.9 16.2 %all_to_all.16 = bf16[64,5,2,128]{3,2,1,0:T(2,128)(2,1)S(1)} all-to-all(bf16[64,5,2,128]{3,2,1,0:T(2,128)(2,1)S(1)} %bitcast.5), channel_id=1, replica_groups=mesh['tm'=8,'azim'=64] {'azim'}, dimensions={0} | all-to-all | bytes 327680 | tf_op jit(solution)/shard_map/all_to_all | solution.py:196
  47.1 0.1 arrange.1
  47.2 0.1 broadcast_in_dim.2
  47.3 11.5 %all_to_all.17.mine_ref = bf16[4,2,320,128]{3,2,1,0:T(8,128)(2,1)S(1)} all-to-all(bf16[4,2,320,128]{3,2,1,0:T(8,128)(2,1)S(1)} %broadcast_in_dim.2), channel_id=1, replica_groups={{0,128,256,384},{64,192,320,448},{1,129,257,385},{65,193,321,449},{2,13..., dimensions={0} | all-to-all | bytes 1310720 | tf_op jit(solution)/shard_map/all_to_all | solution.py:206
  58.7 6.3 %collective-permute-start = (bf16[4,2,320,128]{3,2,1,0:T(8,128)(2,1)S(1)}, bf16[4,2,320,128]{3,2,1,0:T(8,128)(2,1)S(1)}, u32[]{:S(2)}, u32[]{:S(2)}) collective-permute-start(bf16[4,2,320,128]{3,2,1,0:T(8,128)(2,1)S(1)} %all_to_all.17.mine_ref), channel_id=1, source_target_pairs={{0,64},{64,0},{128,192},{192,128},{256,320},{320,256},{384,448},{4... | collective-permute-start | bytes 1966088 | tf_op jit(solution)/shard_map/ppermute | solution.py:209
  65.0 1.8 %own.1 = (f32[2,2,128,1024]{3,2,1,0:T(8,128)}, bf16[2,256,320]{2,1,0:T(8,128)(2,1)S(1)}, f32[2,5,256,128]{3,2,1,0:T(8,128)S(1)}) custom-call(bf16[4,2,320,128]{3,2,1,0:T(8,128)(2,1)S(1)} %all_to_all.17.mine_ref), custom_call_target="tpu_custom_call" | custom-call | tf_op jit(solution)/shard_map/own/pallas_call | solution.py:213
  66.8 0.0 collective-permute-done.theirs_ref
  66.8 2.2 %partner.1 = (f32[2,2,128,1024]{3,2,1,0:T(8,128)}, f32[2,2,128,1024]{3,2,1,0:T(8,128)}) custom-call(bf16[4,2,320,128]{3,2,1,0:T(8,128)(2,1)S(1)} %collective-permute-done.theirs_ref, bf16[2,256,320]{2,1,0:T(8,128)(2,1)S(1)} %get-tuple-element.9.left_ref, f32[2,5,256,128]{3,2,1,0:T(8,128)S(1)} %get-tuple-element.10.next_ref, ...), custom_call_target="tpu_custom_call", output_to_operand_aliasing={{0}: (3, {})} | custom-call | tf_op jit(solution)/shard_map/partner/pallas_call | solution.py:222
Async XLA Ops:
  58.7 8.1 %collective-permute-start = (bf16[4,2,320,128]{3,2,1,0:T(8,128)(2,1)S(1)}, bf16[4,2,320,128]{3,2,1,0:T(8,128)(2,1)S(1)}, u32[]{:S(2)}, u32[]{:S(2)}) collective-permute-start(bf16[4,2,320,128]{3,2,1,0:T(8,128)(2,1)S(1)} %all_to_all.17.mine_ref), channel_id=1, source_target_pairs={{0,64},{64,0},{128,192},{192,128},{256,320},{320,256},{384,448},{4... | collective-permute-start | bytes 1966088 | tf_op jit(solution)/shard_map/ppermute | solution.py:209

commit v5 on v4

--- a/solution.py
+++ b/solution.py
@@ -84,12 +84,10 @@
     o_ref[1] = pltpu.roll(jnp.where(low, second, first), HALF, 1)
 
 
-def blocks_of(left_ref, ref, m):
-    for x in range(0, CHIPS, 2):
-        rows = jnp.concatenate([ref[x, m], ref[x + 1, m]], axis=1)
-        g = jnp.dot(left_ref[m], rows, preferred_element_type=jnp.float32) * jnp.float32(GAIN)
-        yield x, g[:, :LANES]
-        yield x + 1, g[:, LANES:]
+def columns_of(left_ref, ref, m, x):
+    rows = jnp.concatenate([ref[x, m], ref[x + 1, m]], axis=1)
+    g = jnp.dot(left_ref[m], rows, preferred_element_type=jnp.float32) * jnp.float32(GAIN)
+    return g[:, :LANES], g[:, LANES:]
 
 
 def tile_copy(src, dst, m, x, par, sem):
@@ -102,9 +100,24 @@
     ref[m, x, 1] = value[LANES:]
 
 
-def own_kernel(mine_ref, xx_ref, left_ref, next_ref, tile, sems):
+def own_kernel(mine_ref, xx_ref, xy_ref, left_ref, next_ref, tile, zero, sems, zsems):
     tm = lax.axis_index("tm")
     core = lax.rem(tm, 2)
+    zero[...] = jnp.zeros(zero.shape, jnp.float32)
+
+    def blank(j, act):
+        @pl.when(j > tm)
+        def _():
+            for i, dst in enumerate((xx_ref, xy_ref)):
+                act(pltpu.make_async_copy(zero, dst.at[:, :, :, pl.ds(j * LANES, LANES)], zsems.at[i, j]))
+
+    def tiles(m, x, act):
+        @pl.when(2 * x + core <= tm)
+        def _():
+            act(tile_copy(tile, xx_ref, m, x, core, sems.at[m, x]))
+
+    for j in range(1, 2 * CHIPS):
+        blank(j, lambda copy: copy.start())
     even = lax.rem(lax.broadcasted_iota(jnp.int32, (2 * ROWS, LANES), 0), 2) == 0
 
     @pl.loop(0, 2)
@@ -113,46 +126,67 @@
         turned = jnp.where(even, -pltpu.roll(f, 2 * ROWS - 1, 0), pltpu.roll(f, 1, 0))
         left_ref[m, :LANES] = f.T.astype(jnp.bfloat16)
         left_ref[m, LANES:] = turned.T.astype(jnp.bfloat16)
-        for x, block in blocks_of(left_ref, mine_ref, m):
-            store_tile(tile, m, x, jnp.where(2 * x + core <= tm, block, 0.0))
-            tile_copy(tile, xx_ref, m, x, core, sems.at[m, x]).start()
-            next_ref[m, x] = pltpu.roll(block, LANES - 1, 1)
-        next_ref[m, CHIPS] = jnp.zeros((2 * LANES, LANES), jnp.float32)
+        for first in range(0, CHIPS, 2):
+
+            @pl.when(2 * first + core <= tm)
+            def _():
+                for i, block in enumerate(columns_of(left_ref, mine_ref, m, first)):
+                    store_tile(tile, m, first + i, block)
+                    tiles(m, first + i, lambda copy: copy.start())
+                    next_ref[m, first + i] = pltpu.roll(block, LANES - 1, 1)
 
     for m in range(2):
         for x in range(CHIPS):
-            tile_copy(tile, xx_ref, m, x, core, sems.at[m, x]).wait()
-
-
-def partner_kernel(theirs_ref, left_ref, next_ref, old_ref, xx_ref, xy_ref, tile, pair, ynext, sems, ysems):
-    del old_ref
+            tiles(m, x, lambda copy: copy.wait())
+    for j in range(1, 2 * CHIPS):
+        blank(j, lambda copy: copy.wait())
+
+
+def partner_kernel(theirs_ref, left_ref, next_ref, old_xx, old_xy, xx_ref, xy_ref, tile, pair, ynext, sems, ysems):
+    del old_xx, old_xy
     tm = lax.axis_index("tm")
     core = lax.rem(tm, 2)
     other = 1 - core
     inner = lax.broadcasted_iota(jnp.int32, (2 * LANES, LANES), 1) < LANES - 1
 
+    def other_tiles(m, x, act):
+        @pl.when(2 * x + other <= tm)
+        def _():
+            act(tile_copy(tile, xx_ref, m, x, other, sems.at[m, x]))
+            act(tile_copy(pair.at[1], xy_ref, m, x, other, ysems.at[1, m, x]))
+
+    def own_tile(m, x):
+        return tile_copy(pair.at[0], xy_ref, m, x, core, ysems.at[0, m, x])
+
     @pl.loop(0, 2)
     def _(m):
-        for x, block in blocks_of(left_ref, theirs_ref, m):
-            keep = 2 * x + other <= tm
-            store_tile(tile, m, x, jnp.where(keep, block, 0.0))
-            tile_copy(tile, xx_ref, m, x, other, sems.at[m, x]).start()
-            shifted = pltpu.roll(block, LANES - 1, 1)
-            ynext[m, x] = shifted
-            whole = jnp.where(inner, shifted, next_ref[m, x + 1 - core])
-            store_tile(pair.at[1], m, x, jnp.where(keep, whole, 0.0))
-            tile_copy(pair.at[1], xy_ref, m, x, other, ysems.at[1, m, x]).start()
+        for first in range(0, CHIPS, 2):
+
+            @pl.when(2 * first + other <= tm + 1)
+            def _():
+                for i, block in enumerate(columns_of(left_ref, theirs_ref, m, first)):
+                    x = first + i
+                    store_tile(tile, m, x, block)
+                    shifted = pltpu.roll(block, LANES - 1, 1)
+                    ynext[m, x] = shifted
+                    store_tile(pair.at[1], m, x, jnp.where(inner, shifted, next_ref[m, x + 1 - core]))
+                    other_tiles(m, x, lambda copy: copy.start())
+
         ynext[m, CHIPS] = jnp.zeros((2 * LANES, LANES), jnp.float32)
         for x in range(CHIPS):
-            whole = jnp.where(inner, next_ref[m, x], ynext[m, x + core])
-            store_tile(pair.at[0], m, x, jnp.where(2 * x + core <= tm, whole, 0.0))
-            tile_copy(pair.at[0], xy_ref, m, x, core, ysems.at[0, m, x]).start()
+
+            @pl.when(2 * x + core <= tm)
+            def _():
+                store_tile(pair.at[0], m, x, jnp.where(inner, next_ref[m, x], ynext[m, x + core]))
+                own_tile(m, x).start()
 
     for m in range(2):
         for x in range(CHIPS):
-            tile_copy(tile, xx_ref, m, x, other, sems.at[m, x]).wait()
-            tile_copy(pair.at[1], xy_ref, m, x, other, ysems.at[1, m, x]).wait()
-            tile_copy(pair.at[0], xy_ref, m, x, core, ysems.at[0, m, x]).wait()
+            other_tiles(m, x, lambda copy: copy.wait())
+
+            @pl.when(2 * x + core <= tm)
+            def _():
+                own_tile(m, x).wait()
 
 
 def near(array):
@@ -210,19 +244,24 @@
     out = jax.ShapeDtypeStruct((2, 2, LANES, 2 * WIDE), f32)
     tile = pltpu.VMEM((2, CHIPS, 2, LANES, LANES), f32)
     steps = (2, CHIPS + 1, 2 * LANES, LANES)
-    gram_xx, left, after = pl.pallas_call(
+    gram_xx, gram_xy, left, after = pl.pallas_call(
         own_kernel,
-        out_shape=(out, pltpu.VMEM((2, 2 * LANES, 2 * ROWS), bf16), pltpu.VMEM(steps, f32)),
+        out_shape=(out, out, pltpu.VMEM((2, 2 * LANES, 2 * ROWS), bf16), pltpu.VMEM(steps, f32)),
         in_specs=[vmem],
-        out_specs=(hbm, vmem, vmem),
-        scratch_shapes=[tile, pltpu.SemaphoreType.DMA((2, CHIPS))],
+        out_specs=(hbm, hbm, vmem, vmem),
+        scratch_shapes=[
+            tile,
+            pltpu.VMEM((2, 2, LANES, LANES), f32),
+            pltpu.SemaphoreType.DMA((2, CHIPS)),
+            pltpu.SemaphoreType.DMA((2, 2 * CHIPS)),
+        ],
         compiler_params=GRANT,
         name="own",
     )(near(mine))
     return pl.pallas_call(
         partner_kernel,
         out_shape=(out, out),
-        in_specs=[vmem, vmem, vmem, hbm],
+        in_specs=[vmem, vmem, vmem, hbm, hbm],
         out_specs=(hbm, hbm),
         scratch_shapes=[
             tile,
@@ -231,10 +270,10 @@
             pltpu.SemaphoreType.DMA((2, CHIPS)),
             pltpu.SemaphoreType.DMA((2, 2, CHIPS)),
         ],
-        input_output_aliases={3: 0},
+        input_output_aliases={3: 0, 4: 1},
         compiler_params=GRANT,
         name="partner",
-    )(near(theirs), near(left), near(after), gram_xx)
+    )(near(theirs), near(left), near(after), gram_xx, gram_xy)
 
 
 def solution(mesh):

time: 69.3 us -> 68.9 us (level)
  no operation moved by 1% of the time
where the time goes in v5:
time: 68.9 us; the launch traced here: 68.6 us
  blocking collectives  56.4 us (82%)
  starting transfers between devices  6.28 us (9%)
  Pallas kernels  5.2 us (8%)
    all_to_all x1, blocking collectives, body(): lax.all_to_all(send.reshape(PARTS, FIVE, 2, LANES), 'azim', 0, 0, tiled=T...  28.7 us
    all_to_all x1, blocking collectives, body(): lax.all_to_all(spectrum.reshape(PARTS, FIVE, 2, LANES), 'azim', 0, 0, til...  16.2 us
    all_to_all x1, blocking collectives, body(): lax.all_to_all(jnp.broadcast_to(owned[None], (CHIPS,) + owned.shape), 'tm...  11.5 us
    ppermute x1, starting transfers between devices, body(): theirs = lax.ppermute(mine, 'tm', [(i, i ^ 1) for i in range(2 * CHIPS)])  6.28 us
    pallas_call x1, Pallas kernels, body(): pl.pallas_call(own_kernel, out_shape=(out, out, pltpu.VMEM((2, 2 * LANES,...  1.98 us
    pallas_call x1, Pallas kernels, body(): pl.pallas_call(partner_kernel, out_shape=(out, out), in_specs=[vmem, vmem...  1.58 us
  transfers between devices with their start and end apart: 1, of which 0 were waited for; matrix products, arithmetic and copies ran while one was open for 0% of the time, Pallas kernels for 3%

profile of v5, /device:TPU:1, one launch (start us, length us, event | category | flops | bytes accessed | tf_op | source)
XLA Modules:
  0.0 68.6 jit_solution(7690087578225981021)
XLA Ops:
  0.6 1.1 %spread.1 = (bf16[640,128]{1,0:T(8,128)(2,1)S(1)}, bf16[512,128]{1,0:T(8,128)(2,1)S(1)}) custom-call(bf16[4,160,128]{2,1,0:T(8,128)(2,1)} %x_ref.1, bf16[512,128]{1,0:T(8,128)(2,1)} %constant.2.clone.t_ref), custom_call_target="tpu_custom_call" | custom-call | tf_op jit(solution)/shard_map/spread/pallas_call | solution.py:207
  1.8 28.7 %all_to_all.15 = bf16[64,5,2,128]{3,2,1,0:T(2,128)(2,1)S(1)} all-to-all(bf16[64,5,2,128]{3,2,1,0:T(2,128)(2,1)S(1)} %bitcast.7), channel_id=1, replica_groups=mesh['tm'=8,'azim'=64] {'azim'}, dimensions={0} | all-to-all | bytes 327680 | tf_op jit(solution)/shard_map/all_to_all | solution.py:220
  30.4 0.4 transform.1
  30.9 16.2 %all_to_all.16 = bf16[64,5,2,128]{3,2,1,0:T(2,128)(2,1)S(1)} all-to-all(bf16[64,5,2,128]{3,2,1,0:T(2,128)(2,1)S(1)} %bitcast.5), channel_id=1, replica_groups=mesh['tm'=8,'azim'=64] {'azim'}, dimensions={0} | all-to-all | bytes 327680 | tf_op jit(solution)/shard_map/all_to_all | solution.py:230
  47.1 0.1 arrange.1
  47.2 0.1 broadcast_in_dim.2
  47.3 11.5 %all_to_all.17.mine_ref = bf16[4,2,320,128]{3,2,1,0:T(8,128)(2,1)S(1)} all-to-all(bf16[4,2,320,128]{3,2,1,0:T(8,128)(2,1)S(1)} %broadcast_in_dim.2), channel_id=1, replica_groups={{0,128,256,384},{64,192,320,448},{1,129,257,385},{65,193,321,449},{2,13..., dimensions={0} | all-to-all | bytes 1310720 | tf_op jit(solution)/shard_map/all_to_all | solution.py:240
  58.7 6.3 %collective-permute-start = (bf16[4,2,320,128]{3,2,1,0:T(8,128)(2,1)S(1)}, bf16[4,2,320,128]{3,2,1,0:T(8,128)(2,1)S(1)}, u32[]{:S(2)}, u32[]{:S(2)}) collective-permute-start(bf16[4,2,320,128]{3,2,1,0:T(8,128)(2,1)S(1)} %all_to_all.17.mine_ref), channel_id=1, source_target_pairs={{0,64},{64,0},{128,192},{192,128},{256,320},{320,256},{384,448},{4... | collective-permute-start | bytes 1966088 | tf_op jit(solution)/shard_map/ppermute | solution.py:243
  65.0 2.0 %own.1 = (f32[2,2,128,1024]{3,2,1,0:T(8,128)}, f32[2,2,128,1024]{3,2,1,0:T(8,128)}, bf16[2,256,320]{2,1,0:T(8,128)(2,1)S(1)}, f32[2,5,256,128]{3,2,1,0:T(8,128)S(1)}) custom-call(bf16[4,2,320,128]{3,2,1,0:T(8,128)(2,1)S(1)} %all_to_all.17.mine_ref), custom_call_target="tpu_custom_call" | custom-call | tf_op jit(solution)/shard_map/own/pallas_call | solution.py:247
  67.0 0.0 collective-permute-done.theirs_ref
  67.0 1.6 %partner.1 = (f32[2,2,128,1024]{3,2,1,0:T(8,128)}, f32[2,2,128,1024]{3,2,1,0:T(8,128)}) custom-call(bf16[4,2,320,128]{3,2,1,0:T(8,128)(2,1)S(1)} %collective-permute-done.theirs_ref, bf16[2,256,320]{2,1,0:T(8,128)(2,1)S(1)} %get-tuple-element.10.left_ref, ...), custom_call_target="tpu_custom_call", output_to_operand_aliasing={{0}: (3, {}), {1}: (4, {})} | custom-call | tf_op jit(solution)/shard_map/partner/pallas_call | solution.py:261
Async XLA Ops:
  58.7 8.3 %collective-permute-start = (bf16[4,2,320,128]{3,2,1,0:T(8,128)(2,1)S(1)}, bf16[4,2,320,128]{3,2,1,0:T(8,128)(2,1)S(1)}, u32[]{:S(2)}, u32[]{:S(2)}) collective-permute-start(bf16[4,2,320,128]{3,2,1,0:T(8,128)(2,1)S(1)} %all_to_all.17.mine_ref), channel_id=1, source_target_pairs={{0,64},{64,0},{128,192},{192,128},{256,320},{320,256},{384,448},{4... | collective-permute-start | bytes 1966088 | tf_op jit(solution)/shard_map/ppermute | solution.py:243

commit v6 on v5

--- a/solution.py
+++ b/solution.py
@@ -100,24 +100,25 @@
     ref[m, x, 1] = value[LANES:]
 
 
-def own_kernel(mine_ref, xx_ref, xy_ref, left_ref, next_ref, tile, zero, sems, zsems):
+def own_step(mine_ref, xx_ref, xy_ref, left_ref, next_ref, tile, zero, sems, zsems):
     tm = lax.axis_index("tm")
     core = lax.rem(tm, 2)
     zero[...] = jnp.zeros(zero.shape, jnp.float32)
 
-    def blank(j, act):
-        @pl.when(j > tm)
-        def _():
-            for i, dst in enumerate((xx_ref, xy_ref)):
-                act(pltpu.make_async_copy(zero, dst.at[:, :, :, pl.ds(j * LANES, LANES)], zsems.at[i, j]))
-
-    def tiles(m, x, act):
-        @pl.when(2 * x + core <= tm)
-        def _():
-            act(tile_copy(tile, xx_ref, m, x, core, sems.at[m, x]))
-
-    for j in range(1, 2 * CHIPS):
-        blank(j, lambda copy: copy.start())
+    def blank(dst, j, sem):
+        at = pl.multiple_of(j * LANES, LANES)
+        return pltpu.make_async_copy(zero, dst.at[:, :, :, pl.ds(at, LANES)], sem)
+
+    def blanks(act):
+        @pl.loop(tm + 1, 2 * CHIPS)
+        def _(j):
+            act(blank(xy_ref, j, zsems.at[0, j]))
+
+        @pl.loop(lax.div(tm + 1, 2), CHIPS)
+        def _(x):
+            act(blank(xx_ref, 2 * x + 1 - core, zsems.at[1, x]))
+
+    blanks(lambda copy: copy.start())
     even = lax.rem(lax.broadcasted_iota(jnp.int32, (2 * ROWS, LANES), 0), 2) == 0
 
     @pl.loop(0, 2)
@@ -127,19 +128,33 @@
         left_ref[m, :LANES] = f.T.astype(jnp.bfloat16)
         left_ref[m, LANES:] = turned.T.astype(jnp.bfloat16)
         for first in range(0, CHIPS, 2):
-
-            @pl.when(2 * first + core <= tm)
-            def _():
-                for i, block in enumerate(columns_of(left_ref, mine_ref, m, first)):
-                    store_tile(tile, m, first + i, block)
-                    tiles(m, first + i, lambda copy: copy.start())
-                    next_ref[m, first + i] = pltpu.roll(block, LANES - 1, 1)
+            for i, block in enumerate(columns_of(left_ref, mine_ref, m, first)):
+                x = first + i
+                store_tile(tile, m, x, jnp.where(2 * x + core <= tm, block, 0.0))
+                tile_copy(tile, xx_ref, m, x, core, sems.at[m, x]).start()
+                next_ref[m, x] = pltpu.roll(block, LANES - 1, 1)
+        next_ref[m, CHIPS] = jnp.zeros((2 * LANES, LANES), jnp.float32)
 
     for m in range(2):
         for x in range(CHIPS):
-            tiles(m, x, lambda copy: copy.wait())
-    for j in range(1, 2 * CHIPS):
-        blank(j, lambda copy: copy.wait())
+            tile_copy(tile, xx_ref, m, x, core, sems.at[m, x]).wait()
+    blanks(lambda copy: copy.wait())
+
+
+def ahead_kernel(mine_ref, same_ref, *rest):
+    del same_ref
+
+    @pl.when(lax.rem(lax.axis_index("tm"), 2) == 1)
+    def _():
+        own_step(mine_ref, *rest)
+
+
+def behind_kernel(mine_ref, old_xx, old_xy, old_left, old_next, *rest):
+    del old_xx, old_xy, old_left, old_next
+
+    @pl.when(lax.rem(lax.axis_index("tm"), 2) == 0)
+    def _():
+        own_step(mine_ref, *rest)
 
 
 def partner_kernel(theirs_ref, left_ref, next_ref, old_xx, old_xy, xx_ref, xy_ref, tile, pair, ynext, sems, ysems):
@@ -148,12 +163,6 @@
     core = lax.rem(tm, 2)
     other = 1 - core
     inner = lax.broadcasted_iota(jnp.int32, (2 * LANES, LANES), 1) < LANES - 1
-
-    def other_tiles(m, x, act):
-        @pl.when(2 * x + other <= tm)
-        def _():
-            act(tile_copy(tile, xx_ref, m, x, other, sems.at[m, x]))
-            act(tile_copy(pair.at[1], xy_ref, m, x, other, ysems.at[1, m, x]))
 
     def own_tile(m, x):
         return tile_copy(pair.at[0], xy_ref, m, x, core, ysems.at[0, m, x])
@@ -170,7 +179,11 @@
                     shifted = pltpu.roll(block, LANES - 1, 1)
                     ynext[m, x] = shifted
                     store_tile(pair.at[1], m, x, jnp.where(inner, shifted, next_ref[m, x + 1 - core]))
-                    other_tiles(m, x, lambda copy: copy.start())
+
+                    @pl.when(2 * x + other <= tm)
+                    def _():
+                        tile_copy(tile, xx_ref, m, x, other, sems.at[m, x]).start()
+                        tile_copy(pair.at[1], xy_ref, m, x, other, ysems.at[1, m, x]).start()
 
         ynext[m, CHIPS] = jnp.zeros((2 * LANES, LANES), jnp.float32)
         for x in range(CHIPS):
@@ -180,13 +193,16 @@
                 store_tile(pair.at[0], m, x, jnp.where(inner, next_ref[m, x], ynext[m, x + core]))
                 own_tile(m, x).start()
 
-    for m in range(2):
-        for x in range(CHIPS):
-            other_tiles(m, x, lambda copy: copy.wait())
-
-            @pl.when(2 * x + core <= tm)
-            def _():
-                own_tile(m, x).wait()
+    @pl.loop(0, lax.div(tm + 1, 2))
+    def _(x):
+        for m in range(2):
+            tile_copy(tile, xx_ref, m, x, other, sems.at[m, x]).wait()
+            tile_copy(pair.at[1], xy_ref, m, x, other, ysems.at[1, m, x]).wait()
+
+    @pl.loop(0, lax.div(tm, 2) + 1)
+    def _(x):
+        for m in range(2):
+            own_tile(m, x).wait()
 
 
 def near(array):
@@ -240,24 +256,37 @@
     mine = lax.all_to_all(
         jnp.broadcast_to(owned[None], (CHIPS,) + owned.shape), "tm", 0, 0, tiled=True, axis_index_groups=chips
     )
-    theirs = lax.ppermute(mine, "tm", [(i, i ^ 1) for i in range(2 * CHIPS)])
     out = jax.ShapeDtypeStruct((2, 2, LANES, 2 * WIDE), f32)
     tile = pltpu.VMEM((2, CHIPS, 2, LANES, LANES), f32)
     steps = (2, CHIPS + 1, 2 * LANES, LANES)
+    results = (out, out, pltpu.VMEM((2, 2 * LANES, 2 * ROWS), bf16), pltpu.VMEM(steps, f32))
+    scratch = [
+        tile,
+        pltpu.VMEM((2, 2, LANES, LANES), f32),
+        pltpu.SemaphoreType.DMA((2, CHIPS)),
+        pltpu.SemaphoreType.DMA((2, 2 * CHIPS)),
+    ]
+    mine, gram_xx, gram_xy, left, after = pl.pallas_call(
+        ahead_kernel,
+        out_shape=(pltpu.VMEM(mine.shape, bf16),) + results,
+        in_specs=[vmem],
+        out_specs=(vmem, hbm, hbm, vmem, vmem),
+        scratch_shapes=scratch,
+        input_output_aliases={0: 0},
+        compiler_params=GRANT,
+        name="ahead",
+    )(near(mine))
+    theirs = lax.ppermute(mine, "tm", [(i, i ^ 1) for i in range(2 * CHIPS)])
     gram_xx, gram_xy, left, after = pl.pallas_call(
-        own_kernel,
-        out_shape=(out, out, pltpu.VMEM((2, 2 * LANES, 2 * ROWS), bf16), pltpu.VMEM(steps, f32)),
-        in_specs=[vmem],
+        behind_kernel,
+        out_shape=results,
+        in_specs=[vmem, hbm, hbm, vmem, vmem],
         out_specs=(hbm, hbm, vmem, vmem),
-        scratch_shapes=[
-            tile,
-            pltpu.VMEM((2, 2, LANES, LANES), f32),
-            pltpu.SemaphoreType.DMA((2, CHIPS)),
-            pltpu.SemaphoreType.DMA((2, 2 * CHIPS)),
-        ],
-        compiler_params=GRANT,
-        name="own",
-    )(near(mine))
+        scratch_shapes=scratch,
+        input_output_aliases={1: 0, 2: 1, 3: 2, 4: 3},
+        compiler_params=GRANT,
+        name="behind",
+    )(near(mine), gram_xx, gram_xy, near(left), near(after))
     return pl.pallas_call(
         partner_kernel,
         out_shape=(out, out),

time: 68.9 us -> 68.8 us (level)
  starting transfers between devices: 6.28 us -> 4.47 us
  waiting for transfers between devices: 0.01 us -> 1.46 us
    ppermute x1, starting transfers between devices: 6.28 us -> 4.47 us  [body(): theirs = lax.ppermute(mine, 'tm', [(i, i ^ 1) for i in range(2 * CHIPS)])]
    ppermute x1, waiting for transfers between devices: 0.01 us -> 1.46 us  [body(): theirs = lax.ppermute(mine, 'tm', [(i, i ^ 1) for i in range(2 * CHIPS)])]
    pallas_call x1 -> x2, Pallas kernels: 1.98 us -> 2.27 us  [the longest x1 2.04 us: body(): pl.pallas_call(ahead_kernel, out_shape=(pltpu.VMEM(mine.shape, bf16),) +...]
  transfers between devices with their start and end apart: 1 -> 1, of which waited for: 0 -> 1; matrix products, arithmetic and copies ran while one was open for 0% -> 0% of each run, Pallas kernels for 3% -> 0%
where the time goes in v6:
time: 68.8 us; the launch traced here: 68.5 us
  blocking collectives  56.4 us (82%)
  Pallas kernels  5.47 us (8%)
  starting transfers between devices  4.47 us (6%)
  waiting for transfers between devices  1.46 us (2%)
    all_to_all x1, blocking collectives, body(): lax.all_to_all(send.reshape(PARTS, FIVE, 2, LANES), 'azim', 0, 0, tiled=T...  28.7 us
    all_to_all x1, blocking collectives, body(): lax.all_to_all(spectrum.reshape(PARTS, FIVE, 2, LANES), 'azim', 0, 0, til...  16.2 us
    all_to_all x1, blocking collectives, body(): lax.all_to_all(jnp.broadcast_to(owned[None], (CHIPS,) + owned.shape), 'tm...  11.5 us
    ppermute x1, starting transfers between devices, body(): theirs = lax.ppermute(mine, 'tm', [(i, i ^ 1) for i in range(2 * CHIPS)])  4.47 us
    pallas_call x1, Pallas kernels, body(): pl.pallas_call(ahead_kernel, out_shape=(pltpu.VMEM(mine.shape, bf16),) +...  2.04 us
    pallas_call x1, Pallas kernels, body(): pl.pallas_call(partner_kernel, out_shape=(out, out), in_specs=[vmem, vmem...  1.56 us
    ppermute x1, waiting for transfers between devices, body(): theirs = lax.ppermute(mine, 'tm', [(i, i ^ 1) for i in range(2 * CHIPS)])  1.46 us
  transfers between devices with their start and end apart: 1, of which 1 were waited for; matrix products, arithmetic and copies ran while one was open for 0% of the time, Pallas kernels for 0%

profile of v6, /device:TPU:1, one launch (start us, length us, event | category | flops | bytes accessed | tf_op | source)
XLA Modules:
  0.0 68.5 jit_solution(3786453404624393085)
XLA Ops:
  0.6 1.1 %spread.1 = (bf16[640,128]{1,0:T(8,128)(2,1)S(1)}, bf16[512,128]{1,0:T(8,128)(2,1)S(1)}) custom-call(bf16[4,160,128]{2,1,0:T(8,128)(2,1)} %x_ref.1, bf16[512,128]{1,0:T(8,128)(2,1)} %constant.2.clone.t_ref), custom_call_target="tpu_custom_call" | custom-call | tf_op jit(solution)/shard_map/spread/pallas_call | solution.py:223
  1.8 28.7 %all_to_all.15 = bf16[64,5,2,128]{3,2,1,0:T(2,128)(2,1)S(1)} all-to-all(bf16[64,5,2,128]{3,2,1,0:T(2,128)(2,1)S(1)} %bitcast.7), channel_id=1, replica_groups=mesh['tm'=8,'azim'=64] {'azim'}, dimensions={0} | all-to-all | bytes 327680 | tf_op jit(solution)/shard_map/all_to_all | solution.py:236
  30.4 0.4 transform.1
  30.9 16.2 %all_to_all.16 = bf16[64,5,2,128]{3,2,1,0:T(2,128)(2,1)S(1)} all-to-all(bf16[64,5,2,128]{3,2,1,0:T(2,128)(2,1)S(1)} %bitcast.5), channel_id=1, replica_groups=mesh['tm'=8,'azim'=64] {'azim'}, dimensions={0} | all-to-all | bytes 327680 | tf_op jit(solution)/shard_map/all_to_all | solution.py:246
  47.1 0.1 arrange.1
  47.2 0.1 broadcast_in_dim.2
  47.3 11.5 %all_to_all.17.mine_ref = bf16[4,2,320,128]{3,2,1,0:T(8,128)(2,1)S(1)} all-to-all(bf16[4,2,320,128]{3,2,1,0:T(8,128)(2,1)S(1)} %broadcast_in_dim.2), channel_id=1, replica_groups={{0,128,256,384},{64,192,320,448},{1,129,257,385},{65,193,321,449},{2,13..., dimensions={0} | all-to-all | bytes 1310720 | tf_op jit(solution)/shard_map/all_to_all | solution.py:256
  58.7 2.0 %ahead.1 = (bf16[4,2,320,128]{3,2,1,0:T(8,128)(2,1)S(1)}, f32[2,2,128,1024]{3,2,1,0:T(8,128)}, f32[2,2,128,1024]{3,2,1,0:T(8,128)}, bf16[2,256,320]{2,1,0:T(8,128)(2,1)S(1)}, f32[2,5,256,128]{3,2,1,0:T(8,128)S(1)}) custom-call(bf16[4,2,320,128]{3,2,1,0:T(8,128)(2,1)S(1)} %all_to_all.17.mine_ref), custom_call_target="tpu_custom_call", output_to_operand_aliasing={{0}: (0, {})} | custom-call | tf_op jit(solution)/shard_map/ahead/pallas_call | solution.py:269
  60.8 4.5 %collective-permute-start = (bf16[4,2,320,128]{3,2,1,0:T(8,128)(2,1)S(1)}, bf16[4,2,320,128]{3,2,1,0:T(8,128)(2,1)S(1)}, u32[]{:S(2)}, u32[]{:S(2)}) collective-permute-start(bf16[4,2,320,128]{3,2,1,0:T(8,128)(2,1)S(1)} %get-tuple-element.15.mine_ref), channel_id=1, source_target_pairs={{0,64},{64,0},{128,192},{192,128},{256,320},{320,256},{384,448},{4... | collective-permute-start | bytes 1966088 | tf_op jit(solution)/shard_map/ppermute | solution.py:279
  65.3 0.2 behind.1
  65.5 1.5 %collective-permute-done.theirs_ref = bf16[4,2,320,128]{3,2,1,0:T(8,128)(2,1)S(1)} collective-permute-done((bf16[4,2,320,128]{3,2,1,0:T(8,128)(2,1)S(1)}, bf16[4,2,320,128]{3,2,1,0:T(8,128)(2,1)S(1)}, u32[]{:S(2)}, u32[]{:S(2)}) %collective-permute-start) | collective-permute-done | bytes 655392 | tf_op jit(solution)/shard_map/ppermute | solution.py:279
  67.0 1.6 %partner.1 = (f32[2,2,128,1024]{3,2,1,0:T(8,128)}, f32[2,2,128,1024]{3,2,1,0:T(8,128)}) custom-call(bf16[4,2,320,128]{3,2,1,0:T(8,128)(2,1)S(1)} %collective-permute-done.theirs_ref, bf16[2,256,320]{2,1,0:T(8,128)(2,1)S(1)} %get-tuple-element.20.left_ref, ...), custom_call_target="tpu_custom_call", output_to_operand_aliasing={{0}: (3, {}), {1}: (4, {})} | custom-call | tf_op jit(solution)/shard_map/partner/pallas_call | solution.py:290
Async XLA Ops:
  60.8 6.2 %collective-permute-start = (bf16[4,2,320,128]{3,2,1,0:T(8,128)(2,1)S(1)}, bf16[4,2,320,128]{3,2,1,0:T(8,128)(2,1)S(1)}, u32[]{:S(2)}, u32[]{:S(2)}) collective-permute-start(bf16[4,2,320,128]{3,2,1,0:T(8,128)(2,1)S(1)} %get-tuple-element.15.mine_ref), channel_id=1, source_target_pairs={{0,64},{64,0},{128,192},{192,128},{256,320},{320,256},{384,448},{4... | collective-permute-start | bytes 1966088 | tf_op jit(solution)/shard_map/ppermute | solution.py:279

commit v7 on v6

--- a/solution.py
+++ b/solution.py
@@ -92,12 +92,17 @@
 
 def tile_copy(src, dst, m, x, par, sem):
     at = pl.multiple_of((2 * x + par) * LANES, LANES)
-    return pltpu.make_async_copy(src.at[m, x], dst.at[m, :, :, pl.ds(at, LANES)], sem)
+    return pltpu.make_async_copy(src.at[x, m], dst.at[m, :, :, pl.ds(at, LANES)], sem)
+
+
+def both_copy(src, dst, x, par, sem):
+    at = pl.multiple_of((2 * x + par) * LANES, LANES)
+    return pltpu.make_async_copy(src.at[x], dst.at[:, :, :, pl.ds(at, LANES)], sem)
 
 
 def store_tile(ref, m, x, value):
-    ref[m, x, 0] = value[:LANES]
-    ref[m, x, 1] = value[LANES:]
+    ref[x, m, 0] = value[:LANES]
+    ref[x, m, 1] = value[LANES:]
 
 
 def own_step(mine_ref, xx_ref, xy_ref, left_ref, next_ref, tile, zero, sems, zsems):
@@ -164,45 +169,41 @@
     other = 1 - core
     inner = lax.broadcasted_iota(jnp.int32, (2 * LANES, LANES), 1) < LANES - 1
 
-    def own_tile(m, x):
-        return tile_copy(pair.at[0], xy_ref, m, x, core, ysems.at[0, m, x])
-
-    @pl.loop(0, 2)
-    def _(m):
-        for first in range(0, CHIPS, 2):
-
-            @pl.when(2 * first + other <= tm + 1)
-            def _():
+    ynext[:, CHIPS] = jnp.zeros((2, 2 * LANES, LANES), jnp.float32)
+    for first in range(0, CHIPS, 2):
+
+        @pl.when(2 * first + other <= tm + 1)
+        def _():
+            for m in range(2):
                 for i, block in enumerate(columns_of(left_ref, theirs_ref, m, first)):
                     x = first + i
                     store_tile(tile, m, x, block)
                     shifted = pltpu.roll(block, LANES - 1, 1)
                     ynext[m, x] = shifted
                     store_tile(pair.at[1], m, x, jnp.where(inner, shifted, next_ref[m, x + 1 - core]))
-
-                    @pl.when(2 * x + other <= tm)
-                    def _():
-                        tile_copy(tile, xx_ref, m, x, other, sems.at[m, x]).start()
-                        tile_copy(pair.at[1], xy_ref, m, x, other, ysems.at[1, m, x]).start()
-
-        ynext[m, CHIPS] = jnp.zeros((2 * LANES, LANES), jnp.float32)
-        for x in range(CHIPS):
-
-            @pl.when(2 * x + core <= tm)
-            def _():
+            for x in range(first, first + 2):
+
+                @pl.when(2 * x + other <= tm)
+                def _():
+                    both_copy(tile, xx_ref, x, other, sems.at[x]).start()
+                    both_copy(pair.at[1], xy_ref, x, other, ysems.at[1, x]).start()
+
+    for x in range(CHIPS):
+
+        @pl.when(2 * x + core <= tm)
+        def _():
+            for m in range(2):
                 store_tile(pair.at[0], m, x, jnp.where(inner, next_ref[m, x], ynext[m, x + core]))
-                own_tile(m, x).start()
+            both_copy(pair.at[0], xy_ref, x, core, ysems.at[0, x]).start()
 
     @pl.loop(0, lax.div(tm + 1, 2))
     def _(x):
-        for m in range(2):
-            tile_copy(tile, xx_ref, m, x, other, sems.at[m, x]).wait()
-            tile_copy(pair.at[1], xy_ref, m, x, other, ysems.at[1, m, x]).wait()
+        both_copy(tile, xx_ref, x, other, sems.at[x]).wait()
+        both_copy(pair.at[1], xy_ref, x, other, ysems.at[1, x]).wait()
 
     @pl.loop(0, lax.div(tm, 2) + 1)
     def _(x):
-        for m in range(2):
-            own_tile(m, x).wait()
+        both_copy(pair.at[0], xy_ref, x, core, ysems.at[0, x]).wait()
 
 
 def near(array):
@@ -257,7 +258,7 @@
         jnp.broadcast_to(owned[None], (CHIPS,) + owned.shape), "tm", 0, 0, tiled=True, axis_index_groups=chips
     )
     out = jax.ShapeDtypeStruct((2, 2, LANES, 2 * WIDE), f32)
-    tile = pltpu.VMEM((2, CHIPS, 2, LANES, LANES), f32)
+    tile = pltpu.VMEM((CHIPS, 2, 2, LANES, LANES), f32)
     steps = (2, CHIPS + 1, 2 * LANES, LANES)
     results = (out, out, pltpu.VMEM((2, 2 * LANES, 2 * ROWS), bf16), pltpu.VMEM(steps, f32))
     scratch = [
@@ -294,10 +295,10 @@
         out_specs=(hbm, hbm),
         scratch_shapes=[
             tile,
-            pltpu.VMEM((2, 2, CHIPS, 2, LANES, LANES), f32),
+            pltpu.VMEM((2, CHIPS, 2, 2, LANES, LANES), f32),
             pltpu.VMEM(steps, f32),
+            pltpu.SemaphoreType.DMA((CHIPS,)),
             pltpu.SemaphoreType.DMA((2, CHIPS)),
-            pltpu.SemaphoreType.DMA((2, 2, CHIPS)),
         ],
         input_output_aliases={3: 0, 4: 1},
         compiler_params=GRANT,

time: 68.8 us -> 68.6 us (level)
  no operation moved by 1% of the time
where the time goes in v7:
time: 68.6 us; the launch traced here: 68.3 us
  blocking collectives  56.4 us (82%)
  Pallas kernels  5.26 us (8%)
  starting transfers between devices  4.47 us (7%)
  waiting for transfers between devices  1.46 us (2%)
    all_to_all x1, blocking collectives, body(): lax.all_to_all(send.reshape(PARTS, FIVE, 2, LANES), 'azim', 0, 0, tiled=T...  28.7 us
    all_to_all x1, blocking collectives, body(): lax.all_to_all(spectrum.reshape(PARTS, FIVE, 2, LANES), 'azim', 0, 0, til...  16.2 us
    all_to_all x1, blocking collectives, body(): lax.all_to_all(jnp.broadcast_to(owned[None], (CHIPS,) + owned.shape), 'tm...  11.5 us
    ppermute x1, starting transfers between devices, body(): theirs = lax.ppermute(mine, 'tm', [(i, i ^ 1) for i in range(2 * CHIPS)])  4.47 us
    pallas_call x1, Pallas kernels, body(): pl.pallas_call(ahead_kernel, out_shape=(pltpu.VMEM(mine.shape, bf16),) +...  2.04 us
    ppermute x1, waiting for transfers between devices, body(): theirs = lax.ppermute(mine, 'tm', [(i, i ^ 1) for i in range(2 * CHIPS)])  1.46 us
  transfers between devices with their start and end apart: 1, of which 1 were waited for; matrix products, arithmetic and copies ran while one was open for 0% of the time, Pallas kernels for 0%

profile of v7, /device:TPU:1, one launch (start us, length us, event | category | flops | bytes accessed | tf_op | source)
XLA Modules:
  0.0 68.3 jit_solution(7094544392797896673)
XLA Ops:
  0.6 1.1 %spread.1 = (bf16[640,128]{1,0:T(8,128)(2,1)S(1)}, bf16[512,128]{1,0:T(8,128)(2,1)S(1)}) custom-call(bf16[4,160,128]{2,1,0:T(8,128)(2,1)} %x_ref.1, bf16[512,128]{1,0:T(8,128)(2,1)} %constant.2.clone.t_ref), custom_call_target="tpu_custom_call" | custom-call | tf_op jit(solution)/shard_map/spread/pallas_call | solution.py:224
  1.8 28.7 %all_to_all.15 = bf16[64,5,2,128]{3,2,1,0:T(2,128)(2,1)S(1)} all-to-all(bf16[64,5,2,128]{3,2,1,0:T(2,128)(2,1)S(1)} %bitcast.7), channel_id=1, replica_groups=mesh['tm'=8,'azim'=64] {'azim'}, dimensions={0} | all-to-all | bytes 327680 | tf_op jit(solution)/shard_map/all_to_all | solution.py:237
  30.4 0.4 transform.1
  30.9 16.2 %all_to_all.16 = bf16[64,5,2,128]{3,2,1,0:T(2,128)(2,1)S(1)} all-to-all(bf16[64,5,2,128]{3,2,1,0:T(2,128)(2,1)S(1)} %bitcast.5), channel_id=1, replica_groups=mesh['tm'=8,'azim'=64] {'azim'}, dimensions={0} | all-to-all | bytes 327680 | tf_op jit(solution)/shard_map/all_to_all | solution.py:247
  47.1 0.1 arrange.1
  47.2 0.1 broadcast_in_dim.2
  47.3 11.5 %all_to_all.17.mine_ref = bf16[4,2,320,128]{3,2,1,0:T(8,128)(2,1)S(1)} all-to-all(bf16[4,2,320,128]{3,2,1,0:T(8,128)(2,1)S(1)} %broadcast_in_dim.2), channel_id=1, replica_groups={{0,128,256,384},{64,192,320,448},{1,129,257,385},{65,193,321,449},{2,13..., dimensions={0} | all-to-all | bytes 1310720 | tf_op jit(solution)/shard_map/all_to_all | solution.py:257
  58.7 2.0 %ahead.1 = (bf16[4,2,320,128]{3,2,1,0:T(8,128)(2,1)S(1)}, f32[2,2,128,1024]{3,2,1,0:T(8,128)}, f32[2,2,128,1024]{3,2,1,0:T(8,128)}, bf16[2,256,320]{2,1,0:T(8,128)(2,1)S(1)}, f32[2,5,256,128]{3,2,1,0:T(8,128)S(1)}) custom-call(bf16[4,2,320,128]{3,2,1,0:T(8,128)(2,1)S(1)} %all_to_all.17.mine_ref), custom_call_target="tpu_custom_call", output_to_operand_aliasing={{0}: (0, {})} | custom-call | tf_op jit(solution)/shard_map/ahead/pallas_call | solution.py:270
  60.8 4.5 %collective-permute-start = (bf16[4,2,320,128]{3,2,1,0:T(8,128)(2,1)S(1)}, bf16[4,2,320,128]{3,2,1,0:T(8,128)(2,1)S(1)}, u32[]{:S(2)}, u32[]{:S(2)}) collective-permute-start(bf16[4,2,320,128]{3,2,1,0:T(8,128)(2,1)S(1)} %get-tuple-element.15.mine_ref), channel_id=1, source_target_pairs={{0,64},{64,0},{128,192},{192,128},{256,320},{320,256},{384,448},{4... | collective-permute-start | bytes 1966088 | tf_op jit(solution)/shard_map/ppermute | solution.py:280
  65.3 0.2 behind.1
  65.5 1.5 %collective-permute-done.theirs_ref = bf16[4,2,320,128]{3,2,1,0:T(8,128)(2,1)S(1)} collective-permute-done((bf16[4,2,320,128]{3,2,1,0:T(8,128)(2,1)S(1)}, bf16[4,2,320,128]{3,2,1,0:T(8,128)(2,1)S(1)}, u32[]{:S(2)}, u32[]{:S(2)}) %collective-permute-start) | collective-permute-done | bytes 655392 | tf_op jit(solution)/shard_map/ppermute | solution.py:280
  67.0 1.3 %partner.1 = (f32[2,2,128,1024]{3,2,1,0:T(8,128)}, f32[2,2,128,1024]{3,2,1,0:T(8,128)}) custom-call(bf16[4,2,320,128]{3,2,1,0:T(8,128)(2,1)S(1)} %collective-permute-done.theirs_ref, bf16[2,256,320]{2,1,0:T(8,128)(2,1)S(1)} %get-tuple-element.20.left_ref, ...), custom_call_target="tpu_custom_call", output_to_operand_aliasing={{0}: (3, {}), {1}: (4, {})} | custom-call | tf_op jit(solution)/shard_map/partner/pallas_call | solution.py:291
Async XLA Ops:
  60.8 6.2 %collective-permute-start = (bf16[4,2,320,128]{3,2,1,0:T(8,128)(2,1)S(1)}, bf16[4,2,320,128]{3,2,1,0:T(8,128)(2,1)S(1)}, u32[]{:S(2)}, u32[]{:S(2)}) collective-permute-start(bf16[4,2,320,128]{3,2,1,0:T(8,128)(2,1)S(1)} %get-tuple-element.15.mine_ref), channel_id=1, source_target_pairs={{0,64},{64,0},{128,192},{192,128},{256,320},{320,256},{384,448},{4... | collective-permute-start | bytes 1966088 | tf_op jit(solution)/shard_map/ppermute | solution.py:280

commit v8 on v7

--- a/solution.py
+++ b/solution.py
@@ -56,17 +56,22 @@
     two = t_ref[pl.ds(pl.multiple_of(256 * (1 - half), 256), 256)]
     scr_in[...] = x_ref[...].astype(jnp.float32)
     low = low_lanes((LANES, LANES))
-    for r5 in range(FIVE):
-        field = jnp.concatenate(
-            [scr_in[pl.ds(2 * r5 + ahi, PARTS, stride=CELL), :] for ahi in range(2)], axis=0
-        ).astype(jnp.bfloat16)
+    def field_of(r5):
+        parts = [scr_in[pl.ds(2 * r5 + ahi, PARTS, stride=CELL), :] for ahi in range(2)]
+        return jnp.concatenate(parts, axis=0).astype(jnp.bfloat16)
+
+    for base in range(0, FIVE, 2):
+        group = range(base, min(base + 2, FIVE))
+        field = jnp.concatenate([field_of(r5) for r5 in group], axis=1)
         y = jnp.dot(one, field, preferred_element_type=jnp.float32)
         w = jnp.dot(two, field, preferred_element_type=jnp.float32)
-        straight = jnp.where(low, y[0:128], w[128:256])
-        crossed = jnp.where(low, w[0:128], y[128:256])
-        both = straight + pltpu.roll(crossed, HALF, 1)
-        for p in range(2):
-            scr_out[pl.ds(2 * r5 + p, PARTS, stride=CELL), :] = both[64 * p : 64 * p + 64]
+        for i, r5 in enumerate(group):
+            at = slice(i * LANES, (i + 1) * LANES)
+            straight = jnp.where(low, y[0:128, at], w[128:256, at])
+            crossed = jnp.where(low, w[0:128, at], y[128:256, at])
+            both = straight + pltpu.roll(crossed, HALF, 1)
+            for p in range(2):
+                scr_out[pl.ds(2 * r5 + p, PARTS, stride=CELL), :] = both[64 * p : 64 * p + 64]
     o_ref[...] = scr_out[...].astype(jnp.bfloat16)
 
 
@@ -80,8 +85,10 @@
     low = low_lanes((2 * ROWS, LANES))
     first = x_ref[0 : 2 * ROWS]
     second = x_ref[2 * ROWS : 4 * ROWS]
-    o_ref[0] = jnp.where(low, first, second)
-    o_ref[1] = pltpu.roll(jnp.where(low, second, first), HALF, 1)
+    modes = (jnp.where(low, first, second), pltpu.roll(jnp.where(low, second, first), HALF, 1))
+    for x in range(CHIPS):
+        for m in range(2):
+            o_ref[x, m] = modes[m]
 
 
 def columns_of(left_ref, ref, m, x):
@@ -247,16 +254,14 @@
     owned = lax.all_to_all(spectrum.reshape(PARTS, FIVE, 2, LANES), "azim", 0, 0, tiled=True)
     owned = pl.pallas_call(
         arrange_kernel,
-        out_shape=pltpu.VMEM((2, 2 * ROWS, LANES), bf16),
+        out_shape=pltpu.VMEM((CHIPS, 2, 2 * ROWS, LANES), bf16),
         in_specs=[vmem],
         out_specs=vmem,
         compiler_params=GRANT,
         name="arrange",
     )(near(owned.reshape(640, LANES)))
     chips = [[2 * x + c for x in range(CHIPS)] for c in range(2)]
-    mine = lax.all_to_all(
-        jnp.broadcast_to(owned[None], (CHIPS,) + owned.shape), "tm", 0, 0, tiled=True, axis_index_groups=chips
-    )
+    mine = lax.all_to_all(owned, "tm", 0, 0, tiled=True, axis_index_groups=chips)
     out = jax.ShapeDtypeStruct((2, 2, LANES, 2 * WIDE), f32)
     tile = pltpu.VMEM((CHIPS, 2, 2, LANES, LANES), f32)
     steps = (2, CHIPS + 1, 2 * LANES, LANES)

time: 68.6 us -> 68.5 us (level)
  no operation moved by 1% of the time
where the time goes in v8:
time: 68.5 us; the launch traced here: 68.2 us
  blocking collectives  56.3 us (82%)
  Pallas kernels  5.29 us (8%)
  starting transfers between devices  4.47 us (7%)
  waiting for transfers between devices  1.46 us (2%)
    all_to_all x1, blocking collectives, body(): lax.all_to_all(send.reshape(PARTS, FIVE, 2, LANES), 'azim', 0, 0, tiled=T...  28.7 us
    all_to_all x1, blocking collectives, body(): lax.all_to_all(spectrum.reshape(PARTS, FIVE, 2, LANES), 'azim', 0, 0, til...  16.2 us
    all_to_all x1, blocking collectives, body(): lax.all_to_all(owned, 'tm', 0, 0, tiled=True, axis_index_groups=chips)  11.4 us
    ppermute x1, starting transfers between devices, body(): theirs = lax.ppermute(mine, 'tm', [(i, i ^ 1) for i in range(2 * CHIPS)])  4.47 us
    pallas_call x1, Pallas kernels, body(): pl.pallas_call(ahead_kernel, out_shape=(pltpu.VMEM(mine.shape, bf16),) +...  2.04 us
    ppermute x1, waiting for transfers between devices, body(): theirs = lax.ppermute(mine, 'tm', [(i, i ^ 1) for i in range(2 * CHIPS)])  1.46 us
  transfers between devices with their start and end apart: 1, of which 1 were waited for; matrix products, arithmetic and copies ran while one was open for 0% of the time, Pallas kernels for 0%

profile of v8, /device:TPU:1, one launch (start us, length us, event | category | flops | bytes accessed | tf_op | source)
XLA Modules:
  0.0 68.2 jit_solution(8647821411234929418)
XLA Ops:
  0.6 1.1 %spread.1 = (bf16[640,128]{1,0:T(8,128)(2,1)S(1)}, bf16[512,128]{1,0:T(8,128)(2,1)S(1)}) custom-call(bf16[4,160,128]{2,1,0:T(8,128)(2,1)} %x_ref.1, bf16[512,128]{1,0:T(8,128)(2,1)} %constant.2.clone.t_ref), custom_call_target="tpu_custom_call" | custom-call | tf_op jit(solution)/shard_map/spread/pallas_call | solution.py:231
  1.8 28.7 %all_to_all.15 = bf16[64,5,2,128]{3,2,1,0:T(2,128)(2,1)S(1)} all-to-all(bf16[64,5,2,128]{3,2,1,0:T(2,128)(2,1)S(1)} %bitcast.7), channel_id=1, replica_groups=mesh['tm'=8,'azim'=64] {'azim'}, dimensions={0} | all-to-all | bytes 327680 | tf_op jit(solution)/shard_map/all_to_all | solution.py:244
  30.4 0.4 transform.1
  30.9 16.2 %all_to_all.16 = bf16[64,5,2,128]{3,2,1,0:T(2,128)(2,1)S(1)} all-to-all(bf16[64,5,2,128]{3,2,1,0:T(2,128)(2,1)S(1)} %bitcast.5), channel_id=1, replica_groups=mesh['tm'=8,'azim'=64] {'azim'}, dimensions={0} | all-to-all | bytes 327680 | tf_op jit(solution)/shard_map/all_to_all | solution.py:254
  47.1 0.1 arrange.1
  47.2 11.4 %all_to_all.17.mine_ref = bf16[4,2,320,128]{3,2,1,0:T(8,128)(2,1)S(1)} all-to-all(bf16[4,2,320,128]{3,2,1,0:T(8,128)(2,1)S(1)} %arrange.1), channel_id=1, replica_groups={{0,128,256,384},{64,192,320,448},{1,129,257,385},{65,193,321,449},{2,13..., dimensions={0} | all-to-all | bytes 1310720 | tf_op jit(solution)/shard_map/all_to_all | solution.py:264
  58.7 2.0 %ahead.1 = (bf16[4,2,320,128]{3,2,1,0:T(8,128)(2,1)S(1)}, f32[2,2,128,1024]{3,2,1,0:T(8,128)}, f32[2,2,128,1024]{3,2,1,0:T(8,128)}, bf16[2,256,320]{2,1,0:T(8,128)(2,1)S(1)}, f32[2,5,256,128]{3,2,1,0:T(8,128)S(1)}) custom-call(bf16[4,2,320,128]{3,2,1,0:T(8,128)(2,1)S(1)} %all_to_all.17.mine_ref), custom_call_target="tpu_custom_call", output_to_operand_aliasing={{0}: (0, {})} | custom-call | tf_op jit(solution)/shard_map/ahead/pallas_call | solution.py:275
  60.7 4.5 %collective-permute-start = (bf16[4,2,320,128]{3,2,1,0:T(8,128)(2,1)S(1)}, bf16[4,2,320,128]{3,2,1,0:T(8,128)(2,1)S(1)}, u32[]{:S(2)}, u32[]{:S(2)}) collective-permute-start(bf16[4,2,320,128]{3,2,1,0:T(8,128)(2,1)S(1)} %get-tuple-element.15.mine_ref), channel_id=1, source_target_pairs={{0,64},{64,0},{128,192},{192,128},{256,320},{320,256},{384,448},{4... | collective-permute-start | bytes 1966088 | tf_op jit(solution)/shard_map/ppermute | solution.py:285
  65.2 0.2 behind.1
  65.4 1.5 %collective-permute-done.theirs_ref = bf16[4,2,320,128]{3,2,1,0:T(8,128)(2,1)S(1)} collective-permute-done((bf16[4,2,320,128]{3,2,1,0:T(8,128)(2,1)S(1)}, bf16[4,2,320,128]{3,2,1,0:T(8,128)(2,1)S(1)}, u32[]{:S(2)}, u32[]{:S(2)}) %collective-permute-start) | collective-permute-done | bytes 655392 | tf_op jit(solution)/shard_map/ppermute | solution.py:285
  66.9 1.3 %partner.1 = (f32[2,2,128,1024]{3,2,1,0:T(8,128)}, f32[2,2,128,1024]{3,2,1,0:T(8,128)}) custom-call(bf16[4,2,320,128]{3,2,1,0:T(8,128)(2,1)S(1)} %collective-permute-done.theirs_ref, bf16[2,256,320]{2,1,0:T(8,128)(2,1)S(1)} %get-tuple-element.20.left_ref, ...), custom_call_target="tpu_custom_call", output_to_operand_aliasing={{0}: (3, {}), {1}: (4, {})} | custom-call | tf_op jit(solution)/shard_map/partner/pallas_call | solution.py:296
Async XLA Ops:
  60.7 6.2 %collective-permute-start = (bf16[4,2,320,128]{3,2,1,0:T(8,128)(2,1)S(1)}, bf16[4,2,320,128]{3,2,1,0:T(8,128)(2,1)S(1)}, u32[]{:S(2)}, u32[]{:S(2)}) collective-permute-start(bf16[4,2,320,128]{3,2,1,0:T(8,128)(2,1)S(1)} %get-tuple-element.15.mine_ref), channel_id=1, source_target_pairs={{0,64},{64,0},{128,192},{192,128},{256,320},{320,256},{384,448},{4... | collective-permute-start | bytes 1966088 | tf_op jit(solution)/shard_map/ppermute | solution.py:285

commit v9 on v8

--- a/solution.py
+++ b/solution.py
@@ -81,7 +81,52 @@
 GRANT = pltpu.CompilerParams(vmem_limit_bytes=16 << 20)
 
 
-def arrange_kernel(x_ref, o_ref):
+def columns_of(left_ref, ref, m, x):
+    rows = jnp.concatenate([ref[x, m], ref[x + 1, m]], axis=1)
+    g = jnp.dot(left_ref[m], rows, preferred_element_type=jnp.float32) * jnp.float32(GAIN)
+    return g[:, :LANES], g[:, LANES:]
+
+
+def tile_copy(src, dst, m, x, par, sem):
+    at = pl.multiple_of((2 * x + par) * LANES, LANES)
+    return pltpu.make_async_copy(src.at[x, m], dst.at[m, :, :, pl.ds(at, LANES)], sem)
+
+
+def both_copy(src, dst, x, par, sem):
+    at = pl.multiple_of((2 * x + par) * LANES, LANES)
+    return pltpu.make_async_copy(src.at[x], dst.at[:, :, :, pl.ds(at, LANES)], sem)
+
+
+def store_tile(ref, m, x, value):
+    ref[x, m, 0] = value[:LANES]
+    ref[x, m, 1] = value[LANES:]
+
+
+def blanks(zero, xx_ref, xy_ref, zsems, act):
+    tm = lax.axis_index("tm")
+    core = lax.rem(tm, 2)
+
+    def blank(dst, j, sem):
+        at = pl.multiple_of(j * LANES, LANES)
+        return pltpu.make_async_copy(zero, dst.at[:, :, :, pl.ds(at, LANES)], sem)
+
+    @pl.loop(tm + 1, 2 * CHIPS)
+    def _(j):
+        act(blank(xy_ref, j, zsems.at[0, j]))
+
+    @pl.loop(lax.div(tm + 1, 2), CHIPS)
+    def _(x):
+        act(blank(xx_ref, 2 * x + 1 - core, zsems.at[1, x]))
+
+
+def arrange_kernel(x_ref, o_ref, xx_ref, xy_ref, zero, zsems):
+    odd = lax.rem(lax.axis_index("tm"), 2) == 1
+
+    @pl.when(odd)
+    def _():
+        zero[...] = jnp.zeros(zero.shape, jnp.float32)
+        blanks(zero, xx_ref, xy_ref, zsems, lambda copy: copy.start())
+
     low = low_lanes((2 * ROWS, LANES))
     first = x_ref[0 : 2 * ROWS]
     second = x_ref[2 * ROWS : 4 * ROWS]
@@ -90,47 +135,21 @@
         for m in range(2):
             o_ref[x, m] = modes[m]
 
-
-def columns_of(left_ref, ref, m, x):
-    rows = jnp.concatenate([ref[x, m], ref[x + 1, m]], axis=1)
-    g = jnp.dot(left_ref[m], rows, preferred_element_type=jnp.float32) * jnp.float32(GAIN)
-    return g[:, :LANES], g[:, LANES:]
-
-
-def tile_copy(src, dst, m, x, par, sem):
-    at = pl.multiple_of((2 * x + par) * LANES, LANES)
-    return pltpu.make_async_copy(src.at[x, m], dst.at[m, :, :, pl.ds(at, LANES)], sem)
-
-
-def both_copy(src, dst, x, par, sem):
-    at = pl.multiple_of((2 * x + par) * LANES, LANES)
-    return pltpu.make_async_copy(src.at[x], dst.at[:, :, :, pl.ds(at, LANES)], sem)
-
-
-def store_tile(ref, m, x, value):
-    ref[x, m, 0] = value[:LANES]
-    ref[x, m, 1] = value[LANES:]
-
-
-def own_step(mine_ref, xx_ref, xy_ref, left_ref, next_ref, tile, zero, sems, zsems):
+    @pl.when(odd)
+    def _():
+        blanks(zero, xx_ref, xy_ref, zsems, lambda copy: copy.wait())
+
+
+def own_kernel(mine_ref, old_xx, old_xy, xx_ref, xy_ref, left_ref, next_ref, tile, zero, sems, zsems):
+    del old_xx, old_xy
     tm = lax.axis_index("tm")
     core = lax.rem(tm, 2)
-    zero[...] = jnp.zeros(zero.shape, jnp.float32)
-
-    def blank(dst, j, sem):
-        at = pl.multiple_of(j * LANES, LANES)
-        return pltpu.make_async_copy(zero, dst.at[:, :, :, pl.ds(at, LANES)], sem)
-
-    def blanks(act):
-        @pl.loop(tm + 1, 2 * CHIPS)
-        def _(j):
-            act(blank(xy_ref, j, zsems.at[0, j]))
-
-        @pl.loop(lax.div(tm + 1, 2), CHIPS)
-        def _(x):
-            act(blank(xx_ref, 2 * x + 1 - core, zsems.at[1, x]))
-
-    blanks(lambda copy: copy.start())
+
+    @pl.when(core == 0)
+    def _():
+        zero[...] = jnp.zeros(zero.shape, jnp.float32)
+        blanks(zero, xx_ref, xy_ref, zsems, lambda copy: copy.start())
+
     even = lax.rem(lax.broadcasted_iota(jnp.int32, (2 * ROWS, LANES), 0), 2) == 0
 
     @pl.loop(0, 2)
@@ -150,23 +169,10 @@
     for m in range(2):
         for x in range(CHIPS):
             tile_copy(tile, xx_ref, m, x, core, sems.at[m, x]).wait()
-    blanks(lambda copy: copy.wait())
-
-
-def ahead_kernel(mine_ref, same_ref, *rest):
-    del same_ref
-
-    @pl.when(lax.rem(lax.axis_index("tm"), 2) == 1)
+
+    @pl.when(core == 0)
     def _():
-        own_step(mine_ref, *rest)
-
-
-def behind_kernel(mine_ref, old_xx, old_xy, old_left, old_next, *rest):
-    del old_xx, old_xy, old_left, old_next
-
-    @pl.when(lax.rem(lax.axis_index("tm"), 2) == 0)
-    def _():
-        own_step(mine_ref, *rest)
+        blanks(zero, xx_ref, xy_ref, zsems, lambda copy: copy.wait())
 
 
 def partner_kernel(theirs_ref, left_ref, next_ref, old_xx, old_xy, xx_ref, xy_ref, tile, pair, ynext, sems, ysems):
@@ -252,47 +258,32 @@
         name="transform",
     )(near(got.reshape(640, LANES)), near(table))
     owned = lax.all_to_all(spectrum.reshape(PARTS, FIVE, 2, LANES), "azim", 0, 0, tiled=True)
-    owned = pl.pallas_call(
+    out = jax.ShapeDtypeStruct((2, 2, LANES, 2 * WIDE), f32)
+    blank = [pltpu.VMEM((2, 2, LANES, LANES), f32), pltpu.SemaphoreType.DMA((2, 2 * CHIPS))]
+    owned, gram_xx, gram_xy = pl.pallas_call(
         arrange_kernel,
-        out_shape=pltpu.VMEM((CHIPS, 2, 2 * ROWS, LANES), bf16),
+        out_shape=(pltpu.VMEM((CHIPS, 2, 2 * ROWS, LANES), bf16), out, out),
         in_specs=[vmem],
-        out_specs=vmem,
+        out_specs=(vmem, hbm, hbm),
+        scratch_shapes=blank,
         compiler_params=GRANT,
         name="arrange",
     )(near(owned.reshape(640, LANES)))
     chips = [[2 * x + c for x in range(CHIPS)] for c in range(2)]
     mine = lax.all_to_all(owned, "tm", 0, 0, tiled=True, axis_index_groups=chips)
-    out = jax.ShapeDtypeStruct((2, 2, LANES, 2 * WIDE), f32)
+    theirs = lax.ppermute(mine, "tm", [(i, i ^ 1) for i in range(2 * CHIPS)])
     tile = pltpu.VMEM((CHIPS, 2, 2, LANES, LANES), f32)
     steps = (2, CHIPS + 1, 2 * LANES, LANES)
-    results = (out, out, pltpu.VMEM((2, 2 * LANES, 2 * ROWS), bf16), pltpu.VMEM(steps, f32))
-    scratch = [
-        tile,
-        pltpu.VMEM((2, 2, LANES, LANES), f32),
-        pltpu.SemaphoreType.DMA((2, CHIPS)),
-        pltpu.SemaphoreType.DMA((2, 2 * CHIPS)),
-    ]
-    mine, gram_xx, gram_xy, left, after = pl.pallas_call(
-        ahead_kernel,
-        out_shape=(pltpu.VMEM(mine.shape, bf16),) + results,
-        in_specs=[vmem],
-        out_specs=(vmem, hbm, hbm, vmem, vmem),
-        scratch_shapes=scratch,
-        input_output_aliases={0: 0},
-        compiler_params=GRANT,
-        name="ahead",
-    )(near(mine))
-    theirs = lax.ppermute(mine, "tm", [(i, i ^ 1) for i in range(2 * CHIPS)])
     gram_xx, gram_xy, left, after = pl.pallas_call(
-        behind_kernel,
-        out_shape=results,
-        in_specs=[vmem, hbm, hbm, vmem, vmem],
+        own_kernel,
+        out_shape=(out, out, pltpu.VMEM((2, 2 * LANES, 2 * ROWS), bf16), pltpu.VMEM(steps, f32)),
+        in_specs=[vmem, hbm, hbm],
         out_specs=(hbm, hbm, vmem, vmem),
-        scratch_shapes=scratch,
-        input_output_aliases={1: 0, 2: 1, 3: 2, 4: 3},
-        compiler_params=GRANT,
-        name="behind",
-    )(near(mine), gram_xx, gram_xy, near(left), near(after))
+        scratch_shapes=[tile, blank[0], pltpu.SemaphoreType.DMA((2, CHIPS)), blank[1]],
+        input_output_aliases={1: 0, 2: 1},
+        compiler_params=GRANT,
+        name="own",
+    )(near(mine), gram_xx, gram_xy)
     return pl.pallas_call(
         partner_kernel,
         out_shape=(out, out),

time: 68.5 us -> 69.3 us (1.012)
  waiting for transfers between devices: 1.46 us -> 0.01 us
  Pallas kernels: 5.29 us -> 6.4 us
  starting transfers between devices: 4.47 us -> 5.22 us
    ppermute x1, waiting for transfers between devices: 1.46 us -> 0.01 us  [body(): theirs = lax.ppermute(mine, 'tm', [(i, i ^ 1) for i in range(2 * CHIPS)])]
    pallas_call x3 -> x2, Pallas kernels: 2.39 us -> 3.5 us  [the longest x1 1.96 us: body(): pl.pallas_call(own_kernel, out_shape=(out, out, pltpu.VMEM((2, 2 * LANES,...]
    ppermute x1, starting transfers between devices: 4.47 us -> 5.22 us  [body(): theirs = lax.ppermute(mine, 'tm', [(i, i ^ 1) for i in range(2 * CHIPS)])]
  transfers between devices with their start and end apart: 1 -> 1, of which waited for: 1 -> 0; matrix products, arithmetic and copies ran while one was open for 0% -> 0% of each run, Pallas kernels for 0% -> 3%
where the time goes in v9:
time: 69.3 us; the launch traced here: 69 us
  blocking collectives  56.7 us (82%)
  Pallas kernels  6.4 us (9%)
  starting transfers between devices  5.22 us (8%)
    all_to_all x1, blocking collectives, body(): lax.all_to_all(send.reshape(PARTS, FIVE, 2, LANES), 'azim', 0, 0, tiled=T...  28.7 us
    all_to_all x1, blocking collectives, body(): lax.all_to_all(spectrum.reshape(PARTS, FIVE, 2, LANES), 'azim', 0, 0, til...  16.2 us
    all_to_all x1, blocking collectives, body(): lax.all_to_all(owned, 'tm', 0, 0, tiled=True, axis_index_groups=chips)  11.8 us
    ppermute x1, starting transfers between devices, body(): theirs = lax.ppermute(mine, 'tm', [(i, i ^ 1) for i in range(2 * CHIPS)])  5.22 us
    pallas_call x1, Pallas kernels, body(): pl.pallas_call(own_kernel, out_shape=(out, out, pltpu.VMEM((2, 2 * LANES,...  1.96 us
    pallas_call x1, Pallas kernels, body(): pl.pallas_call(arrange_kernel, out_shape=(pltpu.VMEM((CHIPS, 2, 2 * ROWS,...  1.55 us
  transfers between devices with their start and end apart: 1, of which 0 were waited for; matrix products, arithmetic and copies ran while one was open for 0% of the time, Pallas kernels for 3%

profile of v9, /device:TPU:1, one launch (start us, length us, event | category | flops | bytes accessed | tf_op | source)
XLA Modules:
  0.0 69.0 jit_solution(11405242295358328314)
XLA Ops:
  0.6 1.1 %spread.1 = (bf16[640,128]{1,0:T(8,128)(2,1)S(1)}, bf16[512,128]{1,0:T(8,128)(2,1)S(1)}) custom-call(bf16[4,160,128]{2,1,0:T(8,128)(2,1)} %x_ref.1, bf16[512,128]{1,0:T(8,128)(2,1)} %constant.2.clone.t_ref), custom_call_target="tpu_custom_call" | custom-call | tf_op jit(solution)/shard_map/spread/pallas_call | solution.py:237
  1.8 28.7 %all_to_all.15 = bf16[64,5,2,128]{3,2,1,0:T(2,128)(2,1)S(1)} all-to-all(bf16[64,5,2,128]{3,2,1,0:T(2,128)(2,1)S(1)} %bitcast.7), channel_id=1, replica_groups=mesh['tm'=8,'azim'=64] {'azim'}, dimensions={0} | all-to-all | bytes 327680 | tf_op jit(solution)/shard_map/all_to_all | solution.py:250
  30.4 0.4 transform.1
  30.9 16.2 %all_to_all.16 = bf16[64,5,2,128]{3,2,1,0:T(2,128)(2,1)S(1)} all-to-all(bf16[64,5,2,128]{3,2,1,0:T(2,128)(2,1)S(1)} %bitcast.5), channel_id=1, replica_groups=mesh['tm'=8,'azim'=64] {'azim'}, dimensions={0} | all-to-all | bytes 327680 | tf_op jit(solution)/shard_map/all_to_all | solution.py:260
  47.1 1.5 %arrange.1 = (bf16[4,2,320,128]{3,2,1,0:T(8,128)(2,1)S(1)}, f32[2,2,128,1024]{3,2,1,0:T(8,128)}, f32[2,2,128,1024]{3,2,1,0:T(8,128)}) custom-call(bf16[640,128]{1,0:T(8,128)(2,1)S(1)} %bitcast.6), custom_call_target="tpu_custom_call" | custom-call | tf_op jit(solution)/shard_map/arrange/pallas_call | solution.py:263
  48.6 11.8 %all_to_all.17.mine_ref = bf16[4,2,320,128]{3,2,1,0:T(8,128)(2,1)S(1)} all-to-all(bf16[4,2,320,128]{3,2,1,0:T(8,128)(2,1)S(1)} %get-tuple-element.13), channel_id=1, replica_groups={{0,128,256,384},{64,192,320,448},{1,129,257,385},{65,193,321,449},{2,13..., dimensions={0} | all-to-all | bytes 1310720 | tf_op jit(solution)/shard_map/all_to_all | solution.py:273
  60.5 5.2 %collective-permute-start = (bf16[4,2,320,128]{3,2,1,0:T(8,128)(2,1)S(1)}, bf16[4,2,320,128]{3,2,1,0:T(8,128)(2,1)S(1)}, u32[]{:S(2)}, u32[]{:S(2)}) collective-permute-start(bf16[4,2,320,128]{3,2,1,0:T(8,128)(2,1)S(1)} %all_to_all.17.mine_ref), channel_id=1, source_target_pairs={{0,64},{64,0},{128,192},{192,128},{256,320},{320,256},{384,448},{4... | collective-permute-start | bytes 1966088 | tf_op jit(solution)/shard_map/ppermute | solution.py:274
  65.7 2.0 %own.1 = (f32[2,2,128,1024]{3,2,1,0:T(8,128)}, f32[2,2,128,1024]{3,2,1,0:T(8,128)}, bf16[2,256,320]{2,1,0:T(8,128)(2,1)S(1)}, f32[2,5,256,128]{3,2,1,0:T(8,128)S(1)}) custom-call(bf16[4,2,320,128]{3,2,1,0:T(8,128)(2,1)S(1)} %all_to_all.17.mine_ref, f32[2,2,128,1024]{3,2,1,0:T(8,128)} %get-tuple-element.14.old_xx, ...), custom_call_target="tpu_custom_call", output_to_operand_aliasing={{0}: (1, {}), {1}: (2, {})} | custom-call | tf_op jit(solution)/shard_map/own/pallas_call | solution.py:277
  67.6 0.0 collective-permute-done.theirs_ref
  67.7 1.4 %partner.1 = (f32[2,2,128,1024]{3,2,1,0:T(8,128)}, f32[2,2,128,1024]{3,2,1,0:T(8,128)}) custom-call(bf16[4,2,320,128]{3,2,1,0:T(8,128)(2,1)S(1)} %collective-permute-done.theirs_ref, bf16[2,256,320]{2,1,0:T(8,128)(2,1)S(1)} %get-tuple-element.16.left_ref, ...), custom_call_target="tpu_custom_call", output_to_operand_aliasing={{0}: (3, {}), {1}: (4, {})} | custom-call | tf_op jit(solution)/shard_map/partner/pallas_call | solution.py:287
Async XLA Ops:
  60.5 7.2 %collective-permute-start = (bf16[4,2,320,128]{3,2,1,0:T(8,128)(2,1)S(1)}, bf16[4,2,320,128]{3,2,1,0:T(8,128)(2,1)S(1)}, u32[]{:S(2)}, u32[]{:S(2)}) collective-permute-start(bf16[4,2,320,128]{3,2,1,0:T(8,128)(2,1)S(1)} %all_to_all.17.mine_ref), channel_id=1, source_target_pairs={{0,64},{64,0},{128,192},{192,128},{256,320},{320,256},{384,448},{4... | collective-permute-start | bytes 1966088 | tf_op jit(solution)/shard_map/ppermute | solution.py:274

commit v10 on v7

--- a/solution.py
+++ b/solution.py
@@ -80,8 +80,10 @@
     low = low_lanes((2 * ROWS, LANES))
     first = x_ref[0 : 2 * ROWS]
     second = x_ref[2 * ROWS : 4 * ROWS]
-    o_ref[0] = jnp.where(low, first, second)
-    o_ref[1] = pltpu.roll(jnp.where(low, second, first), HALF, 1)
+    modes = (jnp.where(low, first, second), pltpu.roll(jnp.where(low, second, first), HALF, 1))
+    for x in range(CHIPS):
+        for m in range(2):
+            o_ref[x, m] = modes[m]
 
 
 def columns_of(left_ref, ref, m, x):
@@ -247,16 +249,14 @@
     owned = lax.all_to_all(spectrum.reshape(PARTS, FIVE, 2, LANES), "azim", 0, 0, tiled=True)
     owned = pl.pallas_call(
         arrange_kernel,
-        out_shape=pltpu.VMEM((2, 2 * ROWS, LANES), bf16),
+        out_shape=pltpu.VMEM((CHIPS, 2, 2 * ROWS, LANES), bf16),
         in_specs=[vmem],
         out_specs=vmem,
         compiler_params=GRANT,
         name="arrange",
     )(near(owned.reshape(640, LANES)))
     chips = [[2 * x + c for x in range(CHIPS)] for c in range(2)]
-    mine = lax.all_to_all(
-        jnp.broadcast_to(owned[None], (CHIPS,) + owned.shape), "tm", 0, 0, tiled=True, axis_index_groups=chips
-    )
+    mine = lax.all_to_all(owned, "tm", 0, 0, tiled=True, axis_index_groups=chips)
     out = jax.ShapeDtypeStruct((2, 2, LANES, 2 * WIDE), f32)
     tile = pltpu.VMEM((CHIPS, 2, 2, LANES, LANES), f32)
     steps = (2, CHIPS + 1, 2 * LANES, LANES)

time: 68.6 us -> 68.5 us (level)
  no operation moved by 1% of the time
where the time goes in v10:
time: 68.5 us; the launch traced here: 68.2 us
  blocking collectives  56.4 us (82%)
  Pallas kernels  5.28 us (8%)
  starting transfers between devices  4.47 us (7%)
  waiting for transfers between devices  1.46 us (2%)
    all_to_all x1, blocking collectives, body(): lax.all_to_all(send.reshape(PARTS, FIVE, 2, LANES), 'azim', 0, 0, tiled=T...  28.7 us
    all_to_all x1, blocking collectives, body(): lax.all_to_all(spectrum.reshape(PARTS, FIVE, 2, LANES), 'azim', 0, 0, til...  16.2 us
    all_to_all x1, blocking collectives, body(): lax.all_to_all(owned, 'tm', 0, 0, tiled=True, axis_index_groups=chips)  11.5 us
    ppermute x1, starting transfers between devices, body(): theirs = lax.ppermute(mine, 'tm', [(i, i ^ 1) for i in range(2 * CHIPS)])  4.47 us
    pallas_call x1, Pallas kernels, body(): pl.pallas_call(ahead_kernel, out_shape=(pltpu.VMEM(mine.shape, bf16),) +...  2.04 us
    ppermute x1, waiting for transfers between devices, body(): theirs = lax.ppermute(mine, 'tm', [(i, i ^ 1) for i in range(2 * CHIPS)])  1.46 us
  transfers between devices with their start and end apart: 1, of which 1 were waited for; matrix products, arithmetic and copies ran while one was open for 0% of the time, Pallas kernels for 0%

profile of v10, /device:TPU:1, one launch (start us, length us, event | category | flops | bytes accessed | tf_op | source)
XLA Modules:
  0.0 68.2 jit_solution(9612871903335281162)
XLA Ops:
  0.6 1.1 %spread.1 = (bf16[640,128]{1,0:T(8,128)(2,1)S(1)}, bf16[512,128]{1,0:T(8,128)(2,1)S(1)}) custom-call(bf16[4,160,128]{2,1,0:T(8,128)(2,1)} %x_ref.1, bf16[512,128]{1,0:T(8,128)(2,1)} %constant.2.clone.t_ref), custom_call_target="tpu_custom_call" | custom-call | tf_op jit(solution)/shard_map/spread/pallas_call | solution.py:226
  1.8 28.7 %all_to_all.15 = bf16[64,5,2,128]{3,2,1,0:T(2,128)(2,1)S(1)} all-to-all(bf16[64,5,2,128]{3,2,1,0:T(2,128)(2,1)S(1)} %bitcast.7), channel_id=1, replica_groups=mesh['tm'=8,'azim'=64] {'azim'}, dimensions={0} | all-to-all | bytes 327680 | tf_op jit(solution)/shard_map/all_to_all | solution.py:239
  30.4 0.4 transform.1
  30.9 16.2 %all_to_all.16 = bf16[64,5,2,128]{3,2,1,0:T(2,128)(2,1)S(1)} all-to-all(bf16[64,5,2,128]{3,2,1,0:T(2,128)(2,1)S(1)} %bitcast.5), channel_id=1, replica_groups=mesh['tm'=8,'azim'=64] {'azim'}, dimensions={0} | all-to-all | bytes 327680 | tf_op jit(solution)/shard_map/all_to_all | solution.py:249
  47.1 0.1 arrange.1
  47.2 11.5 %all_to_all.17.mine_ref = bf16[4,2,320,128]{3,2,1,0:T(8,128)(2,1)S(1)} all-to-all(bf16[4,2,320,128]{3,2,1,0:T(8,128)(2,1)S(1)} %arrange.1), channel_id=1, replica_groups={{0,128,256,384},{64,192,320,448},{1,129,257,385},{65,193,321,449},{2,13..., dimensions={0} | all-to-all | bytes 1310720 | tf_op jit(solution)/shard_map/all_to_all | solution.py:259
  58.7 2.0 %ahead.1 = (bf16[4,2,320,128]{3,2,1,0:T(8,128)(2,1)S(1)}, f32[2,2,128,1024]{3,2,1,0:T(8,128)}, f32[2,2,128,1024]{3,2,1,0:T(8,128)}, bf16[2,256,320]{2,1,0:T(8,128)(2,1)S(1)}, f32[2,5,256,128]{3,2,1,0:T(8,128)S(1)}) custom-call(bf16[4,2,320,128]{3,2,1,0:T(8,128)(2,1)S(1)} %all_to_all.17.mine_ref), custom_call_target="tpu_custom_call", output_to_operand_aliasing={{0}: (0, {})} | custom-call | tf_op jit(solution)/shard_map/ahead/pallas_call | solution.py:270
  60.7 4.5 %collective-permute-start = (bf16[4,2,320,128]{3,2,1,0:T(8,128)(2,1)S(1)}, bf16[4,2,320,128]{3,2,1,0:T(8,128)(2,1)S(1)}, u32[]{:S(2)}, u32[]{:S(2)}) collective-permute-start(bf16[4,2,320,128]{3,2,1,0:T(8,128)(2,1)S(1)} %get-tuple-element.15.mine_ref), channel_id=1, source_target_pairs={{0,64},{64,0},{128,192},{192,128},{256,320},{320,256},{384,448},{4... | collective-permute-start | bytes 1966088 | tf_op jit(solution)/shard_map/ppermute | solution.py:280
  65.2 0.2 behind.1
  65.4 1.5 %collective-permute-done.theirs_ref = bf16[4,2,320,128]{3,2,1,0:T(8,128)(2,1)S(1)} collective-permute-done((bf16[4,2,320,128]{3,2,1,0:T(8,128)(2,1)S(1)}, bf16[4,2,320,128]{3,2,1,0:T(8,128)(2,1)S(1)}, u32[]{:S(2)}, u32[]{:S(2)}) %collective-permute-start) | collective-permute-done | bytes 655392 | tf_op jit(solution)/shard_map/ppermute | solution.py:280
  66.9 1.3 %partner.1 = (f32[2,2,128,1024]{3,2,1,0:T(8,128)}, f32[2,2,128,1024]{3,2,1,0:T(8,128)}) custom-call(bf16[4,2,320,128]{3,2,1,0:T(8,128)(2,1)S(1)} %collective-permute-done.theirs_ref, bf16[2,256,320]{2,1,0:T(8,128)(2,1)S(1)} %get-tuple-element.20.left_ref, ...), custom_call_target="tpu_custom_call", output_to_operand_aliasing={{0}: (3, {}), {1}: (4, {})} | custom-call | tf_op jit(solution)/shard_map/partner/pallas_call | solution.py:291
Async XLA Ops:
  60.7 6.2 %collective-permute-start = (bf16[4,2,320,128]{3,2,1,0:T(8,128)(2,1)S(1)}, bf16[4,2,320,128]{3,2,1,0:T(8,128)(2,1)S(1)}, u32[]{:S(2)}, u32[]{:S(2)}) collective-permute-start(bf16[4,2,320,128]{3,2,1,0:T(8,128)(2,1)S(1)} %get-tuple-element.15.mine_ref), channel_id=1, source_target_pairs={{0,64},{64,0},{128,192},{192,128},{256,320},{320,256},{384,448},{4... | collective-permute-start | bytes 1966088 | tf_op jit(solution)/shard_map/ppermute | solution.py:280
